TPU v7x, 256 devices: a whole 4x4x8 slice. The times are simulated.
256 devices in a mesh: win: 8 (over z), sec: 32 (over x, y, core).
Axes of the slice: x: 4, y: 4, z: 8, core: 2. Of those that a mesh axis runs over, the one named last changes fastest.
Arguments:
- initial: bfloat16 [5, 16, 24, 512], P(None, 'win'), may hold values from -6 to 6
- props: bfloat16 [32, 8, 2, 256, 256], P('sec'), may hold values from -0.25 to 0.25
- screen: float32 [32, 16, 256], P('sec', 'win'), may hold values from -3.140625 to 3.140625
- links: int32 [32, 16, 6], P('sec', 'win'), may hold values from 0 to 15, as said below
- kinds: int32 [32, 16, 6], P('sec', 'win'), may hold values from 0 to 7
- counts: int32 [32, 16], P('sec', 'win'), may hold values from 1 to 6
Outputs:
- fields: bfloat16 [32, 5, 16, 24, 512], P('sec', None, 'win')
Inputs may be any that keep to these rules, and one draw needn't show every extreme that they name: links[s, w, l] lies within w - 1 to w + 1.
All inputs are finite; a program needn't handle non-finite values.
Results may differ from a plain program's by a relative error of at most 0.033.
Values may be sent and summed in bfloat16 or wider, within the bound.
No kernel may reach another device: no remote copies, remote signals or barrier semaphores. Data moves between devices by JAX's collectives and lax.ppermute only.
A program may use at most 64 MiB of HBM per device.

v0:
```python
import jax
import jax.numpy as jnp
from jax import lax
from jax.sharding import PartitionSpec as P


def with_halo(block, sides, width):
    for axis, dim in sides:
        count = lax.axis_size(axis)
        forward = [(i, i + 1) for i in range(count - 1)]
        backward = [(target, source) for source, target in forward]
        low = lax.ppermute(
            lax.slice_in_dim(block, block.shape[dim] - width, None, axis=dim), axis, forward
        )
        high = lax.ppermute(lax.slice_in_dim(block, 0, width, axis=dim), axis, backward)
        block = jnp.concatenate([low, block, high], axis=dim)
    return block


def shifted(array, axis, by):
    count = lax.axis_size(axis)
    pairs = [(i, i + by) for i in range(count) if 0 <= i + by < count]
    return lax.ppermute(array, axis, pairs)


def local(initial, props, screen, links, kinds, counts):
    coeffs = props.shape[-1]
    entries = props.shape[1]
    section_table = props[0]
    real_part = section_table[:, 0]
    imag_part = section_table[:, 1]
    upper = jnp.concatenate([real_part, imag_part], axis=-1)
    lower = jnp.concatenate([-imag_part, real_part], axis=-1)
    blocks = jnp.concatenate([upper, lower], axis=-2)
    local_windows = links.shape[1]
    list_length = links.shape[2]
    first_window = lax.axis_index("win") * local_windows
    position = first_window - 1 + jnp.arange(local_windows + 2, dtype=jnp.int32)
    count_rows = counts[0]
    weighting = (jnp.arange(list_length)[None, :] < count_rows[:, None]).astype(jnp.float32)
    weighting = weighting * lax.rsqrt(count_rows.astype(jnp.float32))[:, None]
    source_hit = (links[0][:, :, None] == position[None, None, :]).astype(jnp.float32)
    kind_hit = (kinds[0][:, :, None] == jnp.arange(entries)[None, None, :]).astype(jnp.float32)
    selection = jnp.einsum("wl,wlj,wlp->pwj", weighting, source_hit, kind_hit)
    screen_phase = screen[0]
    cosine = jnp.cos(screen_phase)[None, :, None, :]
    sine_part = jnp.sin(screen_phase)[None, :, None, :]

    def advance(padded):
        batch_count = padded.shape[0]
        flat_rows = padded.reshape(-1, 2 * coeffs)
        total = jnp.zeros((batch_count, local_windows) + padded.shape[2:], jnp.float32)
        for entry in range(entries):
            product = jnp.dot(flat_rows, blocks[entry], preferred_element_type=jnp.float32).reshape(
                padded.shape
            )
            total = total + jnp.einsum("wj,bjsd->bwsd", selection[entry], product)
        real_out = total[..., :coeffs]
        imag_out = total[..., coeffs:]
        return jnp.concatenate(
            [real_out * cosine - imag_out * sine_part, real_out * sine_part + imag_out * cosine],
            axis=-1,
        ).astype(jnp.bfloat16)

    section_index = lax.axis_index("sec")
    sections = lax.axis_size("sec")
    fronts = initial.shape[0]

    def tick_step(tick_index, carry):
        received, outputs = carry
        front_index = tick_index - section_index
        active = (front_index >= 0) & (front_index < fronts)
        front_slot = jnp.clip(front_index, 0, fronts - 1)
        entering = lax.dynamic_slice_in_dim(initial, front_slot, 1, 0)
        incoming = jnp.where(section_index == 0, entering, received)
        padded = with_halo(incoming, (("win", 1),), 1)
        advanced = lax.cond(active, advance, lambda unused: jnp.zeros_like(received), padded)
        updated = lax.dynamic_update_slice_in_dim(outputs, advanced, front_slot, 0)
        outputs = jnp.where(active, updated, outputs)
        received = shifted(advanced, "sec", 1)
        return (received, outputs)

    empty_front = jnp.zeros_like(initial[:1])
    final_in, outputs = lax.fori_loop(
        0, sections + fronts - 1, tick_step, (empty_front, jnp.zeros_like(initial))
    )
    return outputs[None]


def solution(mesh):
    placed = (
        P(None, "win", None, None),
        P("sec", None, None, None, None),
        P("sec", "win", None),
        P("sec", "win", None),
        P("sec", "win", None),
        P("sec", "win"),
    )
    return jax.shard_map(
        local,
        mesh=mesh,
        in_specs=placed,
        out_specs=P("sec", None, "win", None, None),
        check_vma=False,
    )
```

profile of v0, /device:TPU:31, one launch (start us, length us, event | category | flops | bytes accessed | tf_op | source)
XLA Modules:
  0.0 736.4 jit_solution(17788916348471021691)
XLA Ops:
  4.9 730.8 %while.16 = (s32[]{:T(128)}, bf16[1,2,24,512]{3,1,2,0:T(2,128)(2,1)S(1)}, bf16[5,2,24,512]{3,2,1,0:T(8,128)(2,1)S(1)}, s32[]{:T(128)}, pred[]{:T(512)}, /*index=...) while((s32[]{:T(128)}, ...), condition=%wide.region_3.4_spmd, body=%wide.region_0.3_spmd.sunk | while | flops 404742144 | bytes 26730900 | solution.py:84
  56.8 5.8 collective-permute-start.1
  71.2 5.8 collective-permute-start.1
  85.6 5.8 collective-permute-start.1
  100.0 5.8 collective-permute-start.1
  114.5 5.8 collective-permute-start.1
  209.2 7.3 collective-permute-done.2
  225.7 7.3 collective-permute-done.2
  242.3 7.3 collective-permute-done.2
  258.8 7.3 collective-permute-done.2
  275.3 7.3 collective-permute-done.2
  291.8 7.3 collective-permute-done.2
  308.4 7.3 collective-permute-done.2
  324.9 7.3 collective-permute-done.2
  341.4 7.3 collective-permute-done.2
  358.0 7.3 collective-permute-done.2
  374.5 7.3 collective-permute-done.2
  391.0 7.3 collective-permute-done.2
  407.5 7.3 collective-permute-done.2
  424.1 7.3 collective-permute-done.2
  440.6 7.3 collective-permute-done.2
  457.1 7.3 collective-permute-done.2
  473.6 145.9 %collective-permute-done.2 = bf16[1,2,24,512]{3,1,2,0:T(2,128)(2,1)S(1)} collective-permute-done((bf16[1,2,24,512]{3,1,2,0:T(2,128)(2,1)S(1)}, bf16[1,2,24,512]{3,1,2,0:T(2,128)(2,1)S(1)}, u32[]{:S(2)}, u32[]{:S(2)}) %collective-permute-start.2) | collective-permute-done | bytes 49184 | tf_op jit(solution)/shard_map/while/body/eval_jaxpr/ppermute | solution.py:23
  627.4 7.9 %conditional.2 = (bf16[1,2,24,512]{3,1,2,0:T(2,128)(2,1)S(1)}) conditional(s32[]{:T(128)} %convert_element_type.30, () %tuple.47, (bf16[1,4,24,512]{3,2,1,0:T(8,128)(2,1)S(1)}, bf16[8,512,512]{2,1,0:T(8,128)(2,1)}, bf16[8,2,4]{2,1,0:T(2,128)(2,1)S(1)}, f32[1,2,1,256]{3,1,2,0:T(2,128)S(1)}, f32[1,2,1,256]{3,1,2,0:T(2,128)S(1)}) %tuple.48), branch_computations={%region_1.1_spmd, %region_2.2_spmd} | conditional | flops 404594688 | bytes 25059364 | solution.py:77
  636.6 7.3 collective-permute-done.2
  651.7 7.9 %conditional.2 = (bf16[1,2,24,512]{3,1,2,0:T(2,128)(2,1)S(1)}) conditional(s32[]{:T(128)} %convert_element_type.30, () %tuple.47, (bf16[1,4,24,512]{3,2,1,0:T(8,128)(2,1)S(1)}, bf16[8,512,512]{2,1,0:T(8,128)(2,1)}, bf16[8,2,4]{2,1,0:T(2,128)(2,1)S(1)}, f32[1,2,1,256]{3,1,2,0:T(2,128)S(1)}, f32[1,2,1,256]{3,1,2,0:T(2,128)S(1)}) %tuple.48), branch_computations={%region_1.1_spmd, %region_2.2_spmd} | conditional | flops 404594688 | bytes 25059364 | solution.py:77
  661.0 7.3 collective-permute-done.2
  676.0 7.9 %conditional.2 = (bf16[1,2,24,512]{3,1,2,0:T(2,128)(2,1)S(1)}) conditional(s32[]{:T(128)} %convert_element_type.30, () %tuple.47, (bf16[1,4,24,512]{3,2,1,0:T(8,128)(2,1)S(1)}, bf16[8,512,512]{2,1,0:T(8,128)(2,1)}, bf16[8,2,4]{2,1,0:T(2,128)(2,1)S(1)}, f32[1,2,1,256]{3,1,2,0:T(2,128)S(1)}, f32[1,2,1,256]{3,1,2,0:T(2,128)S(1)}) %tuple.48), branch_computations={%region_1.1_spmd, %region_2.2_spmd} | conditional | flops 404594688 | bytes 25059364 | solution.py:77
  685.3 7.3 collective-permute-done.2
  700.4 7.9 %conditional.2 = (bf16[1,2,24,512]{3,1,2,0:T(2,128)(2,1)S(1)}) conditional(s32[]{:T(128)} %convert_element_type.30, () %tuple.47, (bf16[1,4,24,512]{3,2,1,0:T(8,128)(2,1)S(1)}, bf16[8,512,512]{2,1,0:T(8,128)(2,1)}, bf16[8,2,4]{2,1,0:T(2,128)(2,1)S(1)}, f32[1,2,1,256]{3,1,2,0:T(2,128)S(1)}, f32[1,2,1,256]{3,1,2,0:T(2,128)S(1)}) %tuple.48), branch_computations={%region_1.1_spmd, %region_2.2_spmd} | conditional | flops 404594688 | bytes 25059364 | solution.py:77
  709.7 7.3 collective-permute-done.2
  724.7 7.9 %conditional.2 = (bf16[1,2,24,512]{3,1,2,0:T(2,128)(2,1)S(1)}) conditional(s32[]{:T(128)} %convert_element_type.30, () %tuple.47, (bf16[1,4,24,512]{3,2,1,0:T(8,128)(2,1)S(1)}, bf16[8,512,512]{2,1,0:T(8,128)(2,1)}, bf16[8,2,4]{2,1,0:T(2,128)(2,1)S(1)}, f32[1,2,1,256]{3,1,2,0:T(2,128)S(1)}, f32[1,2,1,256]{3,1,2,0:T(2,128)S(1)}) %tuple.48), branch_computations={%region_1.1_spmd, %region_2.2_spmd} | conditional | flops 404594688 | bytes 25059364 | solution.py:77
  (629 shorter events, 412.4 us)
Async XLA Ops:
  55.5 7.1 collective-permute-start
  69.9 7.1 collective-permute-start
  84.3 7.1 collective-permute-start
  98.7 7.1 collective-permute-start
  113.2 7.1 collective-permute-start
  127.6 7.1 collective-permute-start
  142.0 7.1 collective-permute-start
  156.4 7.1 collective-permute-start
  170.8 7.1 collective-permute-start
  185.3 7.1 collective-permute-start
  207.8 8.7 %collective-permute-start.2 = (bf16[1,2,24,512]{3,1,2,0:T(2,128)(2,1)S(1)}, bf16[1,2,24,512]{3,1,2,0:T(2,128)(2,1)S(1)}, u32[]{:S(2)}, u32[]{:S(2)}) collective-permute-start(bf16[1,2,24,512]{3,1,2,0:T(2,128)(2,1)S(1)} %get-tuple-element.369), channel_id=1, source_target_pairs={{0,1},{1,2},{2,3},{3,4},{4,5},{5,6},{6,7},{7,8},{8,9},{9,10},{10,1... | collective-permute-start | bytes 147464 | tf_op jit(solution)/shard_map/while/body/eval_jaxpr/ppermute | solution.py:23
  224.3 8.7 %collective-permute-start.2 = (bf16[1,2,24,512]{3,1,2,0:T(2,128)(2,1)S(1)}, bf16[1,2,24,512]{3,1,2,0:T(2,128)(2,1)S(1)}, u32[]{:S(2)}, u32[]{:S(2)}) collective-permute-start(bf16[1,2,24,512]{3,1,2,0:T(2,128)(2,1)S(1)} %get-tuple-element.369), channel_id=1, source_target_pairs={{0,1},{1,2},{2,3},{3,4},{4,5},{5,6},{6,7},{7,8},{8,9},{9,10},{10,1... | collective-permute-start | bytes 147464 | tf_op jit(solution)/shard_map/while/body/eval_jaxpr/ppermute | solution.py:23
  233.1 6.8 collective-permute-start
  240.9 8.7 %collective-permute-start.2 = (bf16[1,2,24,512]{3,1,2,0:T(2,128)(2,1)S(1)}, bf16[1,2,24,512]{3,1,2,0:T(2,128)(2,1)S(1)}, u32[]{:S(2)}, u32[]{:S(2)}) collective-permute-start(bf16[1,2,24,512]{3,1,2,0:T(2,128)(2,1)S(1)} %get-tuple-element.369), channel_id=1, source_target_pairs={{0,1},{1,2},{2,3},{3,4},{4,5},{5,6},{6,7},{7,8},{8,9},{9,10},{10,1... | collective-permute-start | bytes 147464 | tf_op jit(solution)/shard_map/while/body/eval_jaxpr/ppermute | solution.py:23
  257.4 8.7 %collective-permute-start.2 = (bf16[1,2,24,512]{3,1,2,0:T(2,128)(2,1)S(1)}, bf16[1,2,24,512]{3,1,2,0:T(2,128)(2,1)S(1)}, u32[]{:S(2)}, u32[]{:S(2)}) collective-permute-start(bf16[1,2,24,512]{3,1,2,0:T(2,128)(2,1)S(1)} %get-tuple-element.369), channel_id=1, source_target_pairs={{0,1},{1,2},{2,3},{3,4},{4,5},{5,6},{6,7},{7,8},{8,9},{9,10},{10,1... | collective-permute-start | bytes 147464 | tf_op jit(solution)/shard_map/while/body/eval_jaxpr/ppermute | solution.py:23
  273.9 8.7 %collective-permute-start.2 = (bf16[1,2,24,512]{3,1,2,0:T(2,128)(2,1)S(1)}, bf16[1,2,24,512]{3,1,2,0:T(2,128)(2,1)S(1)}, u32[]{:S(2)}, u32[]{:S(2)}) collective-permute-start(bf16[1,2,24,512]{3,1,2,0:T(2,128)(2,1)S(1)} %get-tuple-element.369), channel_id=1, source_target_pairs={{0,1},{1,2},{2,3},{3,4},{4,5},{5,6},{6,7},{7,8},{8,9},{9,10},{10,1... | collective-permute-start | bytes 147464 | tf_op jit(solution)/shard_map/while/body/eval_jaxpr/ppermute | solution.py:23
  290.4 8.7 %collective-permute-start.2 = (bf16[1,2,24,512]{3,1,2,0:T(2,128)(2,1)S(1)}, bf16[1,2,24,512]{3,1,2,0:T(2,128)(2,1)S(1)}, u32[]{:S(2)}, u32[]{:S(2)}) collective-permute-start(bf16[1,2,24,512]{3,1,2,0:T(2,128)(2,1)S(1)} %get-tuple-element.369), channel_id=1, source_target_pairs={{0,1},{1,2},{2,3},{3,4},{4,5},{5,6},{6,7},{7,8},{8,9},{9,10},{10,1... | collective-permute-start | bytes 147464 | tf_op jit(solution)/shard_map/while/body/eval_jaxpr/ppermute | solution.py:23
  307.0 8.7 %collective-permute-start.2 = (bf16[1,2,24,512]{3,1,2,0:T(2,128)(2,1)S(1)}, bf16[1,2,24,512]{3,1,2,0:T(2,128)(2,1)S(1)}, u32[]{:S(2)}, u32[]{:S(2)}) collective-permute-start(bf16[1,2,24,512]{3,1,2,0:T(2,128)(2,1)S(1)} %get-tuple-element.369), channel_id=1, source_target_pairs={{0,1},{1,2},{2,3},{3,4},{4,5},{5,6},{6,7},{7,8},{8,9},{9,10},{10,1... | collective-permute-start | bytes 147464 | tf_op jit(solution)/shard_map/while/body/eval_jaxpr/ppermute | solution.py:23
  323.5 8.7 %collective-permute-start.2 = (bf16[1,2,24,512]{3,1,2,0:T(2,128)(2,1)S(1)}, bf16[1,2,24,512]{3,1,2,0:T(2,128)(2,1)S(1)}, u32[]{:S(2)}, u32[]{:S(2)}) collective-permute-start(bf16[1,2,24,512]{3,1,2,0:T(2,128)(2,1)S(1)} %get-tuple-element.369), channel_id=1, source_target_pairs={{0,1},{1,2},{2,3},{3,4},{4,5},{5,6},{6,7},{7,8},{8,9},{9,10},{10,1... | collective-permute-start | bytes 147464 | tf_op jit(solution)/shard_map/while/body/eval_jaxpr/ppermute | solution.py:23
  340.0 8.7 %collective-permute-start.2 = (bf16[1,2,24,512]{3,1,2,0:T(2,128)(2,1)S(1)}, bf16[1,2,24,512]{3,1,2,0:T(2,128)(2,1)S(1)}, u32[]{:S(2)}, u32[]{:S(2)}) collective-permute-start(bf16[1,2,24,512]{3,1,2,0:T(2,128)(2,1)S(1)} %get-tuple-element.369), channel_id=1, source_target_pairs={{0,1},{1,2},{2,3},{3,4},{4,5},{5,6},{6,7},{7,8},{8,9},{9,10},{10,1... | collective-permute-start | bytes 147464 | tf_op jit(solution)/shard_map/while/body/eval_jaxpr/ppermute | solution.py:23
  356.6 8.7 %collective-permute-start.2 = (bf16[1,2,24,512]{3,1,2,0:T(2,128)(2,1)S(1)}, bf16[1,2,24,512]{3,1,2,0:T(2,128)(2,1)S(1)}, u32[]{:S(2)}, u32[]{:S(2)}) collective-permute-start(bf16[1,2,24,512]{3,1,2,0:T(2,128)(2,1)S(1)} %get-tuple-element.369), channel_id=1, source_target_pairs={{0,1},{1,2},{2,3},{3,4},{4,5},{5,6},{6,7},{7,8},{8,9},{9,10},{10,1... | collective-permute-start | bytes 147464 | tf_op jit(solution)/shard_map/while/body/eval_jaxpr/ppermute | solution.py:23
  373.1 8.7 %collective-permute-start.2 = (bf16[1,2,24,512]{3,1,2,0:T(2,128)(2,1)S(1)}, bf16[1,2,24,512]{3,1,2,0:T(2,128)(2,1)S(1)}, u32[]{:S(2)}, u32[]{:S(2)}) collective-permute-start(bf16[1,2,24,512]{3,1,2,0:T(2,128)(2,1)S(1)} %get-tuple-element.369), channel_id=1, source_target_pairs={{0,1},{1,2},{2,3},{3,4},{4,5},{5,6},{6,7},{7,8},{8,9},{9,10},{10,1... | collective-permute-start | bytes 147464 | tf_op jit(solution)/shard_map/while/body/eval_jaxpr/ppermute | solution.py:23
  389.6 8.7 %collective-permute-start.2 = (bf16[1,2,24,512]{3,1,2,0:T(2,128)(2,1)S(1)}, bf16[1,2,24,512]{3,1,2,0:T(2,128)(2,1)S(1)}, u32[]{:S(2)}, u32[]{:S(2)}) collective-permute-start(bf16[1,2,24,512]{3,1,2,0:T(2,128)(2,1)S(1)} %get-tuple-element.369), channel_id=1, source_target_pairs={{0,1},{1,2},{2,3},{3,4},{4,5},{5,6},{6,7},{7,8},{8,9},{9,10},{10,1... | collective-permute-start | bytes 147464 | tf_op jit(solution)/shard_map/while/body/eval_jaxpr/ppermute | solution.py:23
  406.1 8.7 %collective-permute-start.2 = (bf16[1,2,24,512]{3,1,2,0:T(2,128)(2,1)S(1)}, bf16[1,2,24,512]{3,1,2,0:T(2,128)(2,1)S(1)}, u32[]{:S(2)}, u32[]{:S(2)}) collective-permute-start(bf16[1,2,24,512]{3,1,2,0:T(2,128)(2,1)S(1)} %get-tuple-element.369), channel_id=1, source_target_pairs={{0,1},{1,2},{2,3},{3,4},{4,5},{5,6},{6,7},{7,8},{8,9},{9,10},{10,1... | collective-permute-start | bytes 147464 | tf_op jit(solution)/shard_map/while/body/eval_jaxpr/ppermute | solution.py:23
  422.7 8.7 %collective-permute-start.2 = (bf16[1,2,24,512]{3,1,2,0:T(2,128)(2,1)S(1)}, bf16[1,2,24,512]{3,1,2,0:T(2,128)(2,1)S(1)}, u32[]{:S(2)}, u32[]{:S(2)}) collective-permute-start(bf16[1,2,24,512]{3,1,2,0:T(2,128)(2,1)S(1)} %get-tuple-element.369), channel_id=1, source_target_pairs={{0,1},{1,2},{2,3},{3,4},{4,5},{5,6},{6,7},{7,8},{8,9},{9,10},{10,1... | collective-permute-start | bytes 147464 | tf_op jit(solution)/shard_map/while/body/eval_jaxpr/ppermute | solution.py:23
  439.2 8.7 %collective-permute-start.2 = (bf16[1,2,24,512]{3,1,2,0:T(2,128)(2,1)S(1)}, bf16[1,2,24,512]{3,1,2,0:T(2,128)(2,1)S(1)}, u32[]{:S(2)}, u32[]{:S(2)}) collective-permute-start(bf16[1,2,24,512]{3,1,2,0:T(2,128)(2,1)S(1)} %get-tuple-element.369), channel_id=1, source_target_pairs={{0,1},{1,2},{2,3},{3,4},{4,5},{5,6},{6,7},{7,8},{8,9},{9,10},{10,1... | collective-permute-start | bytes 147464 | tf_op jit(solution)/shard_map/while/body/eval_jaxpr/ppermute | solution.py:23
  455.7 8.7 %collective-permute-start.2 = (bf16[1,2,24,512]{3,1,2,0:T(2,128)(2,1)S(1)}, bf16[1,2,24,512]{3,1,2,0:T(2,128)(2,1)S(1)}, u32[]{:S(2)}, u32[]{:S(2)}) collective-permute-start(bf16[1,2,24,512]{3,1,2,0:T(2,128)(2,1)S(1)} %get-tuple-element.369), channel_id=1, source_target_pairs={{0,1},{1,2},{2,3},{3,4},{4,5},{5,6},{6,7},{7,8},{8,9},{9,10},{10,1... | collective-permute-start | bytes 147464 | tf_op jit(solution)/shard_map/while/body/eval_jaxpr/ppermute | solution.py:23
  472.3 147.3 %collective-permute-start.2 = (bf16[1,2,24,512]{3,1,2,0:T(2,128)(2,1)S(1)}, bf16[1,2,24,512]{3,1,2,0:T(2,128)(2,1)S(1)}, u32[]{:S(2)}, u32[]{:S(2)}) collective-permute-start(bf16[1,2,24,512]{3,1,2,0:T(2,128)(2,1)S(1)} %get-tuple-element.369), channel_id=1, source_target_pairs={{0,1},{1,2},{2,3},{3,4},{4,5},{5,6},{6,7},{7,8},{8,9},{9,10},{10,1... | collective-permute-start | bytes 147464 | tf_op jit(solution)/shard_map/while/body/eval_jaxpr/ppermute | solution.py:23
  635.2 8.7 %collective-permute-start.2 = (bf16[1,2,24,512]{3,1,2,0:T(2,128)(2,1)S(1)}, bf16[1,2,24,512]{3,1,2,0:T(2,128)(2,1)S(1)}, u32[]{:S(2)}, u32[]{:S(2)}) collective-permute-start(bf16[1,2,24,512]{3,1,2,0:T(2,128)(2,1)S(1)} %get-tuple-element.369), channel_id=1, source_target_pairs={{0,1},{1,2},{2,3},{3,4},{4,5},{5,6},{6,7},{7,8},{8,9},{9,10},{10,1... | collective-permute-start | bytes 147464 | tf_op jit(solution)/shard_map/while/body/eval_jaxpr/ppermute | solution.py:23
  659.6 8.7 %collective-permute-start.2 = (bf16[1,2,24,512]{3,1,2,0:T(2,128)(2,1)S(1)}, bf16[1,2,24,512]{3,1,2,0:T(2,128)(2,1)S(1)}, u32[]{:S(2)}, u32[]{:S(2)}) collective-permute-start(bf16[1,2,24,512]{3,1,2,0:T(2,128)(2,1)S(1)} %get-tuple-element.369), channel_id=1, source_target_pairs={{0,1},{1,2},{2,3},{3,4},{4,5},{5,6},{6,7},{7,8},{8,9},{9,10},{10,1... | collective-permute-start | bytes 147464 | tf_op jit(solution)/shard_map/while/body/eval_jaxpr/ppermute | solution.py:23
  683.9 8.7 %collective-permute-start.2 = (bf16[1,2,24,512]{3,1,2,0:T(2,128)(2,1)S(1)}, bf16[1,2,24,512]{3,1,2,0:T(2,128)(2,1)S(1)}, u32[]{:S(2)}, u32[]{:S(2)}) collective-permute-start(bf16[1,2,24,512]{3,1,2,0:T(2,128)(2,1)S(1)} %get-tuple-element.369), channel_id=1, source_target_pairs={{0,1},{1,2},{2,3},{3,4},{4,5},{5,6},{6,7},{7,8},{8,9},{9,10},{10,1... | collective-permute-start | bytes 147464 | tf_op jit(solution)/shard_map/while/body/eval_jaxpr/ppermute | solution.py:23
  708.3 8.7 %collective-permute-start.2 = (bf16[1,2,24,512]{3,1,2,0:T(2,128)(2,1)S(1)}, bf16[1,2,24,512]{3,1,2,0:T(2,128)(2,1)S(1)}, u32[]{:S(2)}, u32[]{:S(2)}) collective-permute-start(bf16[1,2,24,512]{3,1,2,0:T(2,128)(2,1)S(1)} %get-tuple-element.369), channel_id=1, source_target_pairs={{0,1},{1,2},{2,3},{3,4},{4,5},{5,6},{6,7},{7,8},{8,9},{9,10},{10,1... | collective-permute-start | bytes 147464 | tf_op jit(solution)/shard_map/while/body/eval_jaxpr/ppermute | solution.py:23
  (87 other events, 528.2 us)
where the time goes:
time: 745 us; the launch traced here: 736 us
  waiting for transfers between devices  392 us (53%)
  starting transfers between devices  289 us (39%)
  matrix products  38.2 us (5%)
    ppermute x36, waiting for transfers between devices, shifted(): return lax.ppermute(array, axis, pairs)  360 us
    ppermute x36, starting transfers between devices, with_halo(): lax.ppermute(lax.slice_in_dim(block, block.shape[dim] - width, None, axis...  196 us
    ppermute x36, starting transfers between devices, with_halo(): lax.ppermute(lax.slice_in_dim(block, 0, width, axis=dim), axis, backward)  46.5 us
    ppermute x36, starting transfers between devices, shifted(): return lax.ppermute(array, axis, pairs)  46.5 us
    ppermute x36, waiting for transfers between devices, with_halo(): lax.ppermute(lax.slice_in_dim(block, block.shape[dim] - width, None, axis...  31.9 us
    dot_general x40, matrix products, advance(): jnp.dot(flat_rows, blocks[entry], preferred_element_type=jnp.float32)  30.5 us
  transfers between devices with their start and end apart: 108, of which 72 were waited for; matrix products, arithmetic and copies ran while one was open for 0% of the time, Pallas kernels for 0%

commit v1 on v0

v1 whole, which is shorter than its diff:
```python
import functools

import jax
import jax.numpy as jnp
from jax import lax
from jax.experimental import pallas as pl
from jax.experimental.pallas import tpu as pltpu
from jax.sharding import PartitionSpec as P

ROWS = 8
LANES = 128
VMEM = pl.BlockSpec(memory_space=pltpu.VMEM)
SMEM = pl.BlockSpec(memory_space=pltpu.SMEM)
ANY = pl.BlockSpec(memory_space=pl.ANY)
LIMIT = pltpu.CompilerParams(vmem_limit_bytes=16 << 20)


def pack_kernel(entries, initial_ref, screen_ref, links_ref, kinds_ref, counts_ref, out_ref):
    fronts, own_windows, sources, width = initial_ref.shape
    core = lax.axis_index("sec") % 2
    first = lax.axis_index("win") * own_windows
    members = out_ref.shape[0]
    list_length = links_ref.shape[-1]
    per_front = sources // ROWS
    lane = lax.broadcasted_iota(jnp.int32, (1, width), 1)
    trig_rows, hit_rows = [], []
    for w in range(own_windows):
        count = counts_ref[0, w]
        scale = lax.rsqrt(jnp.full((1, width // 2), count, jnp.int32).astype(jnp.float32))
        angle = screen_ref[0, w : w + 1, :]
        trig = jnp.concatenate([jnp.cos(angle) * scale, jnp.sin(angle) * scale], axis=1)
        high = trig.astype(jnp.bfloat16)
        trig_rows += [high, (trig - high.astype(jnp.float32)).astype(jnp.bfloat16)]
        hits = jnp.zeros((1, width), jnp.float32)
        for l in range(list_length):
            spot = kinds_ref[0, w, l] * 3 + links_ref[0, w, l] - (first + w) + 1
            hits = hits + jnp.where((lane == spot) & (l < count), 1.0, 0.0)
        hit_rows.append(hits.astype(jnp.bfloat16))
    spare = jnp.zeros((ROWS - 3 * own_windows, width), jnp.bfloat16)
    tables = jnp.concatenate(trig_rows + hit_rows + [spare], axis=0)
    for member in range(members):
        if member < fronts * per_front:
            f, j = divmod(member, per_front)
            out_ref[member, :ROWS] = initial_ref[f, core, j * ROWS : (j + 1) * ROWS]
        else:
            out_ref[member, :ROWS] = jnp.zeros((ROWS, width), jnp.bfloat16)
        out_ref[member, ROWS:] = tables


def unpack_kernel(entries, coeffs, received_ref, field_ref, mix_ref, cs_ref, ds_ref):
    columns = received_ref.shape[0] // 2
    for z in range(columns):
        for core in range(2):
            block = received_ref[2 * z + core]
            window = 2 * z + core
            field_ref[window * ROWS : (window + 1) * ROWS] = block[:ROWS]
            wide = block.astype(jnp.float32)
            for w in range(2):
                at = pl.ds((2 * z + w) * ROWS, ROWS)
                trig = wide[ROWS + 2 * w : ROWS + 2 * w + 1] + wide[ROWS + 2 * w + 1 : ROWS + 2 * w + 2]
                cs_ref[core, at, :] = jnp.broadcast_to(trig[:, :coeffs], (ROWS, coeffs))
                ds_ref[core, at, :] = jnp.broadcast_to(trig[:, coeffs:], (ROWS, coeffs))
                hits = wide[ROWS + 4 + w : ROWS + 5 + w]
                for spot in range(3 * entries):
                    mix_ref[core, spot, at, :] = jnp.broadcast_to(
                        hits[:, spot : spot + 1], (ROWS, LANES)
                    ).astype(jnp.bfloat16)


def order_kernel(own_ref, other_ref, out_ref, sems):
    core = lax.axis_index("sec") % 2
    a = pltpu.make_async_copy(own_ref, out_ref.at[core], sems.at[0])
    b = pltpu.make_async_copy(other_ref, out_ref.at[1 - core], sems.at[1])
    a.start()
    b.start()
    a.wait()
    b.wait()


def stage_kernel(turn, entries, coeffs, x_ref, w_ref, mix_ref, cs_ref, ds_ref, kept_ref, y_ref, out_ref):
    del kept_ref
    points = x_ref.shape[0]
    pairs, sections, group, width = out_ref.shape
    repeat = width // LANES

    @pl.when(lax.axis_index("sec") // 2 == turn)
    def _():
        y_ref[...] = x_ref[...]
        zero = jnp.zeros((ROWS, width), jnp.float32)

        def one(section, carry):
            field = y_ref[...].astype(jnp.float32)
            low = jnp.concatenate([zero, field[:-ROWS]], axis=0)
            high = jnp.concatenate([field[ROWS:], zero], axis=0)
            tops, bottoms = [], []
            for entry in range(entries):
                hits = [
                    jnp.concatenate([mix_ref[section, 3 * entry + j]] * repeat, axis=1).astype(jnp.float32)
                    for j in range(3)
                ]
                mixed = (hits[0] * low + hits[1] * field + hits[2] * high).astype(jnp.bfloat16)
                re, im = mixed[:, :coeffs], mixed[:, coeffs:]
                tops += [re, -im]
                bottoms += [im, re]
            weights = w_ref[section]
            re = jnp.dot(jnp.concatenate(tops, axis=1), weights, preferred_element_type=jnp.float32)
            im = jnp.dot(jnp.concatenate(bottoms, axis=1), weights, preferred_element_type=jnp.float32)
            cs, ds = cs_ref[section], ds_ref[section]
            field = jnp.concatenate([re * cs - im * ds, re * ds + im * cs], axis=1).astype(jnp.bfloat16)
            y_ref[...] = field
            for pair in range(pairs):
                out_ref[pair, section] = field[pair * group : (pair + 1) * group]
            return carry

        lax.fori_loop(0, sections, one, 0)


def local(initial, props, screen, links, kinds, counts):
    fronts, own_windows, sources, width = initial.shape
    coeffs = width // 2
    entries = props.shape[1]
    columns = lax.axis_size("win")
    sections = lax.axis_size("sec")
    chips = sections // 2
    windows = own_windows * columns
    members = 2 * columns
    points = windows * ROWS
    used = fronts * sources // ROWS
    bf16, f32 = jnp.bfloat16, jnp.float32
    groups = [
        [w * sections + 2 * c + k for w in range(columns) for k in range(2)] for c in range(chips)
    ]

    own = props.reshape(entries * 2 * coeffs, coeffs)
    other = lax.ppermute(own, "sec", [(s, s ^ 1) for s in range(sections)])
    weights = pl.pallas_call(
        order_kernel,
        out_shape=jax.ShapeDtypeStruct((2,) + own.shape, bf16),
        in_specs=[ANY, ANY],
        out_specs=VMEM,
        scratch_shapes=[pltpu.SemaphoreType.DMA((2,))],
        compiler_params=LIMIT,
        name="order",
    )(own, other)

    payload = pl.pallas_call(
        functools.partial(pack_kernel, entries),
        out_shape=jax.ShapeDtypeStruct((members, 2 * ROWS, width), bf16),
        in_specs=[VMEM, VMEM, SMEM, SMEM, SMEM],
        out_specs=VMEM,
        compiler_params=LIMIT,
        name="pack",
    )(initial, screen, links, kinds, counts)
    received = lax.all_to_all(payload, ("win", "sec"), 0, 0, axis_index_groups=groups, tiled=True)
    field, mixing, cs, ds = pl.pallas_call(
        functools.partial(unpack_kernel, entries, coeffs),
        out_shape=(
            jax.ShapeDtypeStruct((points, width), bf16),
            jax.ShapeDtypeStruct((2, 3 * entries, points, LANES), bf16),
            jax.ShapeDtypeStruct((2, points, coeffs), f32),
            jax.ShapeDtypeStruct((2, points, coeffs), f32),
        ),
        in_specs=[VMEM],
        out_specs=(VMEM,) * 4,
        compiler_params=LIMIT,
        name="unpack",
    )(received)

    kept = jnp.zeros((columns, 2, own_windows * ROWS, width), bf16)
    for turn in range(chips):
        field, kept = pl.pallas_call(
            functools.partial(stage_kernel, turn, entries, coeffs),
            out_shape=(jax.ShapeDtypeStruct(field.shape, bf16), jax.ShapeDtypeStruct(kept.shape, bf16)),
            in_specs=[VMEM] * 6,
            out_specs=(VMEM, VMEM),
            input_output_aliases={5: 1},
            cost_estimate=pl.CostEstimate(
                flops=16 * entries * points * coeffs * coeffs, bytes_accessed=weights.size * 2, transcendentals=0
            ),
            compiler_params=LIMIT,
            name="stage",
        )(field, weights, mixing, cs, ds, kept)
        if turn + 1 < chips:
            field = lax.ppermute(field, "sec", [(2 * turn + k, 2 * turn + 2 + k) for k in range(2)])

    fields = lax.all_to_all(
        kept.reshape(members, own_windows * ROWS, width), ("win", "sec"), 0, 0, axis_index_groups=groups, tiled=True
    )
    fields = fields[:used].reshape(fronts, sources // ROWS, own_windows, ROWS, width)
    return fields.transpose(0, 2, 1, 3, 4).reshape(initial.shape)[None]


def solution(mesh):
    placed = (
        P(None, "win", None, None),
        P("sec", None, None, None, None),
        P("sec", "win", None),
        P("sec", "win", None),
        P("sec", "win", None),
        P("sec", "win"),
    )
    return jax.shard_map(
        local,
        mesh=mesh,
        in_specs=placed,
        out_specs=P("sec", None, "win", None, None),
        check_vma=False,
    )
```

time: 745 us -> 149 us (0.20); the launches traced: 736 us -> 149 us
  waiting for transfers between devices: 392 us -> 80.6 us
  starting transfers between devices: 289 us -> 11.3 us
  blocking collectives: 0 us -> 46.3 us
  matrix products: 38.2 us -> 0 us
    ppermute x108 -> x16, waiting for transfers between devices: 392 us -> 80.6 us  [the longest x15 80.6 us: local(): lax.ppermute(field, 'sec', [(2 * turn + k, 2 * turn + 2 + k) for k in ran...]
    ppermute x108 -> x16, starting transfers between devices: 289 us -> 11.3 us  [the longest x15 10.7 us: local(): lax.ppermute(field, 'sec', [(2 * turn + k, 2 * turn + 2 + k) for k in ran...]
    all_to_all x0 -> x2, blocking collectives: none -> 46.3 us  [the longest x1 26.2 us: local(): lax.all_to_all(kept.reshape(members, own_windows * ROWS, width), ('win',...]
    dot_general x81 -> x0, matrix products: 38.2 us -> none  [the longest x40 30.5 us: advance(): jnp.dot(flat_rows, blocks[entry], preferred_element_type=jnp.float32)]
  transfers between devices with their start and end apart: 108 -> 16, of which waited for: 72 -> 1; matrix products, arithmetic and copies ran while one was open for 0% -> 0% of each run, Pallas kernels for 0% -> 1%
where the time goes in v1:
time: 149 us
  waiting for transfers between devices  80.6 us (54%)
  blocking collectives  46.3 us (31%)
  starting transfers between devices  11.3 us (8%)
  local copies, waits for them, and re-layouts  5.97 us (4%)
  Pallas kernels  4.04 us (3%)
    ppermute x15, waiting for transfers between devices, local(): lax.ppermute(field, 'sec', [(2 * turn + k, 2 * turn + 2 + k) for k in ran...  80.6 us
    all_to_all x1, blocking collectives, local(): lax.all_to_all(kept.reshape(members, own_windows * ROWS, width), ('win',...  26.2 us
    all_to_all x1, blocking collectives, local(): lax.all_to_all(payload, ('win', 'sec'), 0, 0, axis_index_groups=groups, t...  20.1 us
    ppermute x15, starting transfers between devices, local(): lax.ppermute(field, 'sec', [(2 * turn + k, 2 * turn + 2 + k) for k in ran...  10.7 us
    unnamed x12, local copies, waits for them, and re-layouts  5.22 us
  transfers between devices with their start and end apart: 16, of which 1 were waited for; matrix products, arithmetic and copies ran while one was open for 0% of the time, Pallas kernels for 1%

profile of v1, /device:TPU:31, one launch (start us, length us, event | category | flops | bytes accessed | tf_op | source)
XLA Modules:
  0.0 148.7 jit_solution(6491738503877061955)
XLA Ops:
  0.0 0.7 collective-permute-start
  0.7 0.9 copy-done.1
  1.6 0.7 copy-done.2
  2.3 0.7 copy-done.3
  3.0 0.7 copy-done.4
  3.7 0.7 copy-done.5
  4.3 0.6 pack.1
  5.0 20.1 %all_to_all.10.received_ref = bf16[16,16,512]{2,1,0:T(8,128)(2,1)S(1)} all-to-all(bf16[16,16,512]{2,1,0:T(8,128)(2,1)S(1)} %pack.1), channel_id=1, replica_groups={{0,1,32,33,64,65,96,97,128,129,160,161,192,193,224,225},{2,3,34,35,66,6..., dimensions={0} | all-to-all | bytes 524288 | tf_op jit(solution)/shard_map/all_to_all | solution.py:154
  25.1 0.7 unpack.1
  25.8 0.0 copy-start
  25.8 1.6 %copy-done = bf16[1,8,2,256,256]{4,3,2,1,0:T(8,128)(2,1)S(1)} copy-done((bf16[1,8,2,256,256]{4,3,2,1,0:T(8,128)(2,1)S(1)}, bf16[1,8,2,256,256]{4,3,2,1,0:T(8,128)(2,1)}, u32[]{:S(2)}) %copy-start) | copy-done | bytes 2097176
  27.3 0.3 order.1.w_ref
  27.7 0.7 collective-permute-start.1
  28.4 0.0 collective-permute-done.1.x_ref
  28.4 0.7 collective-permute-start.2
  29.1 0.7 collective-permute-start.3
  29.9 0.7 collective-permute-start.4
  30.6 0.7 collective-permute-start.5
  31.3 0.7 collective-permute-start.6
  32.0 0.7 collective-permute-start.7
  32.7 0.7 collective-permute-start.8
  33.4 0.7 collective-permute-start.9
  34.2 0.7 collective-permute-start.10
  34.9 0.7 collective-permute-start.11
  35.6 0.7 collective-permute-start.12
  36.3 0.7 collective-permute-start.13
  37.0 0.7 collective-permute-start.14
  37.7 1.3 collective-permute-start.15
  39.0 80.6 %collective-permute-done.15.x_ref = bf16[128,512]{1,0:T(8,128)(2,1)S(1)} collective-permute-done((bf16[128,512]{1,0:T(8,128)(2,1)S(1)}, bf16[128,512]{1,0:T(8,128)(2,1)S(1)}, u32[]{:S(2)}, u32[]{:S(2)}) %collective-permute-start.15) | collective-permute-done | bytes 131104 | tf_op jit(solution)/shard_map/ppermute | solution.py:184
  119.6 2.1 %stage.31 = (bf16[128,512]{1,0:T(8,128)(2,1)}, bf16[8,2,16,512]{3,2,1,0:T(8,128)(2,1)S(1)}) custom-call(bf16[128,512]{1,0:T(8,128)(2,1)S(1)} %collective-permute-done.15.x_ref, bf16[2,4096,256]{2,1,0:T(8,128)(2,1)S(1)} %order.1.w_ref, bf16[2,24,128,128]{3,2,1,0:T(8,128)(2,1)S(1)} %get-tuple-element.41.mix_ref, ...), custom_call_target="tpu_custom_call", output_to_operand_aliasing={{1}: (5, {})} | custom-call | flops 1073741824 | bytes 4194304 | tf_op jit(solution)/shard_map/stage/pallas_call | solution.py:171
  121.7 26.2 %all_to_all.11 = bf16[16,16,512]{2,1,0:T(8,128)(2,1)S(1)} all-to-all(bf16[16,16,512]{2,1,0:T(8,128)(2,1)S(1)} %bitcast.8), channel_id=1, replica_groups={{0,1,32,33,64,65,96,97,128,129,160,161,192,193,224,225},{2,3,34,35,66,6..., dimensions={0} | all-to-all | bytes 524288 | tf_op jit(solution)/shard_map/all_to_all | solution.py:186
  148.0 0.7 copy.25
  (36 shorter events, 0.4 us)
Async XLA Ops:
  0.0 25.7 %collective-permute-start = (bf16[4096,256]{1,0:T(8,128)(2,1)}, bf16[4096,256]{1,0:T(8,128)(2,1)S(1)}, u32[]{:S(2)}, u32[]{:S(2)}) collective-permute-start(bf16[4096,256]{1,0:T(8,128)(2,1)} %bitcast.9), channel_id=1, source_target_pairs={{0,1},{1,0},{2,3},{3,2},{4,5},{5,4},{6,7},{7,6},{8,9},{9,8},{10,11... | collective-permute-start | bytes 6291464 | tf_op jit(solution)/shard_map/ppermute | solution.py:135
  0.7 0.9 copy-start.1
  1.6 0.7 copy-start.2
  2.3 0.7 copy-start.3
  3.0 0.7 copy-start.4
  3.7 0.7 copy-start.5
  25.8 1.6 %copy-start = (bf16[1,8,2,256,256]{4,3,2,1,0:T(8,128)(2,1)S(1)}, bf16[1,8,2,256,256]{4,3,2,1,0:T(8,128)(2,1)}, u32[]{:S(2)}) copy-start(bf16[1,8,2,256,256]{4,3,2,1,0:T(8,128)(2,1)} %param.7) | copy-start | bytes 6291460
  27.7 0.7 collective-permute-start.1
  28.4 0.7 collective-permute-start.2
  29.1 0.7 collective-permute-start.3
  29.9 0.7 collective-permute-start.4
  30.6 0.7 collective-permute-start.5
  31.3 0.7 collective-permute-start.6
  32.0 0.7 collective-permute-start.7
  32.7 0.7 collective-permute-start.8
  33.4 0.7 collective-permute-start.9
  34.2 0.7 collective-permute-start.10
  34.9 0.7 collective-permute-start.11
  35.6 0.7 collective-permute-start.12
  36.3 0.7 collective-permute-start.13
  37.0 0.7 collective-permute-start.14
  37.7 81.9 %collective-permute-start.15 = (bf16[128,512]{1,0:T(8,128)(2,1)S(1)}, bf16[128,512]{1,0:T(8,128)(2,1)S(1)}, u32[]{:S(2)}, u32[]{:S(2)}) collective-permute-start(bf16[128,512]{1,0:T(8,128)(2,1)S(1)} %get-tuple-element.72), channel_id=1, source_target_pairs={{28,30},{29,31},{60,62},{61,63},{92,94},{93,95},{124,126},{125,127... | collective-permute-start | bytes 393224 | tf_op jit(solution)/shard_map/ppermute | solution.py:184

commit v2 on v1

v2 whole, which is shorter than its diff:
```python
import functools

import jax
import jax.numpy as jnp
from jax import lax
from jax.experimental import pallas as pl
from jax.experimental.pallas import tpu as pltpu
from jax.sharding import PartitionSpec as P

ROWS = 8
LANES = 128
CHUNKS = 2
UNITS = 2
VMEM = pl.BlockSpec(memory_space=pltpu.VMEM)
HBM = pl.BlockSpec(memory_space=pltpu.HBM)
LIMIT = pltpu.CompilerParams(vmem_limit_bytes=16 << 20)


def pack_kernel(
    entries,
    initial_hbm, screen_hbm, links_hbm, kinds_hbm, counts_hbm, own_hbm, out_ref, weights_ref,
    initial_ref, screen_ref, links_ref, kinds_ref, counts_ref, sems,
):
    copies = [
        pltpu.make_async_copy(source, target, sems.at[i])
        for i, (source, target) in enumerate(
            (
                (counts_hbm, counts_ref),
                (kinds_hbm, kinds_ref),
                (links_hbm, links_ref),
                (screen_hbm, screen_ref),
                (initial_hbm, initial_ref),
                (own_hbm, weights_ref.at[lax.axis_index("sec") % 2]),
            )
        )
    ]
    for copy in copies:
        copy.start()
    for copy in copies[:-1]:
        copy.wait()
    fronts, own_windows, sources, width = initial_ref.shape
    core = lax.axis_index("sec") % 2
    first = lax.axis_index("win") * own_windows
    members = out_ref.shape[0]
    list_length = links_ref.shape[-1]
    per_front = sources // ROWS
    lane = lax.broadcasted_iota(jnp.int32, (1, width), 1)
    trig_rows, hit_rows = [], []
    for w in range(own_windows):
        count = counts_ref[0, w]
        scale = lax.rsqrt(jnp.full((1, width // 2), count, jnp.int32).astype(jnp.float32))
        angle = screen_ref[0, w : w + 1, :]
        trig = jnp.concatenate([jnp.cos(angle) * scale, jnp.sin(angle) * scale], axis=1)
        high = trig.astype(jnp.bfloat16)
        trig_rows += [high, (trig - high.astype(jnp.float32)).astype(jnp.bfloat16)]
        hits = jnp.zeros((1, width), jnp.float32)
        for l in range(list_length):
            spot = kinds_ref[0, w, l] * 3 + links_ref[0, w, l] - (first + w) + 1
            hits = hits + jnp.where((lane == spot) & (l < count), 1.0, 0.0)
        hit_rows.append(hits.astype(jnp.bfloat16))
    spare = jnp.zeros((ROWS - 3 * own_windows, width), jnp.bfloat16)
    tables = jnp.concatenate(trig_rows + hit_rows + [spare], axis=0)
    for member in range(members):
        if member < fronts * per_front:
            f, j = divmod(member, per_front)
            out_ref[member, :ROWS] = initial_ref[f, core, j * ROWS : (j + 1) * ROWS]
        else:
            out_ref[member, :ROWS] = jnp.zeros((ROWS, width), jnp.bfloat16)
        out_ref[member, ROWS:] = tables
    copies[-1].wait()


def unpack_kernel(entries, coeffs, received_ref, other_ref, field_refs, mix_ref, cs_ref, ds_ref, weights_ref, sem):
    copy = pltpu.make_async_copy(other_ref, weights_ref.at[1 - lax.axis_index("sec") % 2], sem)
    copy.start()
    columns = received_ref.shape[0] // 2
    own_windows = 2
    part = ROWS // len(field_refs)
    for z in range(columns):
        blocks = [received_ref[2 * z + core].astype(jnp.float32) for core in range(2)]
        at = pl.ds(own_windows * part * z, own_windows * part)
        for chunk, field_ref in enumerate(field_refs):
            rows = [block[chunk * part : (chunk + 1) * part] for block in blocks]
            field_ref[at, :] = jnp.concatenate(rows, axis=0).astype(jnp.bfloat16)
        for core in range(2):
            trigs, hits = [], []
            for w in range(own_windows):
                row = ROWS + 2 * w
                trig = blocks[core][row : row + 1] + blocks[core][row + 1 : row + 2]
                trigs.append(jnp.broadcast_to(trig, (part, 2 * coeffs)))
                row = ROWS + 2 * own_windows + w
                hits.append(jnp.broadcast_to(blocks[core][row : row + 1, :LANES], (part, LANES)))
            trig = jnp.concatenate(trigs, axis=0)
            cs_ref[core, at, :] = trig[:, :coeffs]
            ds_ref[core, at, :] = trig[:, coeffs:]
            hit = jnp.concatenate(hits, axis=0)
            for spot in range(3 * entries):
                mix_ref[core, spot, at, :] = jnp.broadcast_to(hit[:, spot : spot + 1], (own_windows * part, LANES))
    copy.wait()


def repack_kernel(got_ref, out_ref):
    fronts, own_windows, sources, width = out_ref.shape
    per_front = sources // ROWS
    chunks = got_ref.shape[1] // (own_windows * ROWS // CHUNKS)
    part = ROWS // chunks
    for f in range(fronts):
        for j in range(per_front):
            block = got_ref[f * per_front + j].astype(jnp.float32)
            for w in range(own_windows):
                rows = [block[(c * own_windows + w) * part : (c * own_windows + w + 1) * part] for c in range(chunks)]
                out_ref[f, w, j * ROWS : (j + 1) * ROWS] = jnp.concatenate(rows, axis=0).astype(jnp.bfloat16)


def stage_kernel(turn, chunk, entries, coeffs, x_ref, w_ref, mix_ref, cs_ref, ds_ref, y_ref, out_ref, *sums):
    points, width = x_ref.shape
    pairs, sections, group, _ = out_ref.shape
    step = ROWS // CHUNKS
    group = group // CHUNKS
    repeat = width // LANES

    @pl.when(lax.axis_index("sec") // 2 == turn)
    def _():
        y_ref[...] = x_ref[...]

        def one(section, carry):
            field = y_ref[...].astype(jnp.float32)
            low = pltpu.roll(field, step, 0)
            high = pltpu.roll(field, points - step, 0)
            for entry in range(entries):
                unit = entry % UNITS
                hits = [jnp.concatenate([mix_ref[section, 3 * entry + j]] * repeat, axis=1) for j in range(3)]
                mixed = (hits[0] * low + hits[1] * field + hits[2] * high).astype(jnp.bfloat16)
                re, im = mixed[:, :coeffs], mixed[:, coeffs:]
                for part in range(2):
                    at = pl.ds((2 * entry + part) * coeffs, coeffs)
                    pltpu.matmul_push_rhs(w_ref[section, at, :], part, unit)
                pltpu.matmul_acc_lhs(sums[2 * unit], re, 0)
                pltpu.matmul_acc_lhs(sums[2 * unit + 1], im)
                pltpu.matmul_acc_lhs(sums[2 * unit], -im, 1)
                pltpu.matmul_acc_lhs(sums[2 * unit + 1], re)
            re = pltpu.matmul_pop(sums[0]) + pltpu.matmul_pop(sums[2])
            im = pltpu.matmul_pop(sums[1]) + pltpu.matmul_pop(sums[3])
            cs, ds = cs_ref[section], ds_ref[section]
            field = jnp.concatenate([re * cs - im * ds, re * ds + im * cs], axis=1).astype(jnp.bfloat16)
            y_ref[...] = field
            for pair in range(pairs):
                out_ref[pair, section, chunk * group : (chunk + 1) * group] = field[pair * group : (pair + 1) * group]
            return carry

        lax.fori_loop(0, sections, one, 0)


def stage(turn, chunk, entries, coeffs, field, weights, mixing, cs, ds, kept):
    flops = 16 * entries * field.shape[0] * coeffs * coeffs

    def body(x_ref, w_ref, mix_ref, cs_ref, ds_ref, kept_ref, y_ref, out_ref):
        sums = [pltpu.ACC(unit)((field.shape[0], coeffs), jnp.float32) for unit in range(UNITS) for _ in range(2)]
        run = functools.partial(
            stage_kernel, turn, chunk, entries, coeffs, x_ref, w_ref, mix_ref, cs_ref, ds_ref, y_ref, out_ref
        )
        pl.run_scoped(run, *sums)

    return pl.pallas_call(
        body,
        out_shape=(jax.ShapeDtypeStruct(field.shape, field.dtype), jax.ShapeDtypeStruct(kept.shape, kept.dtype)),
        in_specs=[VMEM] * 6,
        out_specs=(VMEM, VMEM),
        input_output_aliases={5: 1},
        cost_estimate=pl.CostEstimate(flops=flops, bytes_accessed=weights.size * 2, transcendentals=0),
        compiler_params=LIMIT,
        name="stage",
    )(field, weights, mixing, cs, ds, kept)


def local(initial, props, screen, links, kinds, counts):
    fronts, own_windows, sources, width = initial.shape
    coeffs = width // 2
    entries = props.shape[1]
    columns = lax.axis_size("win")
    sections = lax.axis_size("sec")
    chips = sections // 2
    windows = own_windows * columns
    members = 2 * columns
    points = windows * ROWS
    used = fronts * sources // ROWS
    bf16, f32 = jnp.bfloat16, jnp.float32
    groups = [
        [w * sections + 2 * c + k for w in range(columns) for k in range(2)] for c in range(chips)
    ]

    own = props.reshape(entries * 2 * coeffs, coeffs)
    other = lax.ppermute(own, "sec", [(s, s ^ 1) for s in range(sections)])

    payload, weights = pl.pallas_call(
        functools.partial(pack_kernel, entries),
        out_shape=(
            jax.ShapeDtypeStruct((members, 2 * ROWS, width), bf16),
            jax.ShapeDtypeStruct((2,) + own.shape, bf16),
        ),
        in_specs=[HBM] * 6,
        out_specs=(VMEM, VMEM),
        scratch_shapes=[
            pltpu.VMEM(initial.shape, initial.dtype),
            pltpu.VMEM(screen.shape, screen.dtype),
            pltpu.SMEM(links.shape, links.dtype),
            pltpu.SMEM(kinds.shape, kinds.dtype),
            pltpu.SMEM(counts.shape, counts.dtype),
            pltpu.SemaphoreType.DMA((6,)),
        ],
        compiler_params=LIMIT,
        name="pack",
    )(*[pltpu.with_memory_space_constraint(a, pltpu.HBM) for a in (initial, screen, links, kinds, counts, own)])
    received = lax.all_to_all(payload, ("win", "sec"), 0, 0, axis_index_groups=groups, tiled=True)
    part = points // CHUNKS

    def unpack(received_ref, other_ref, weights_in_ref, *refs):
        unpack_kernel(entries, coeffs, received_ref, other_ref, refs[:CHUNKS], *refs[CHUNKS:])

    *chunks, mixing, cs, ds, weights = pl.pallas_call(
        unpack,
        out_shape=(jax.ShapeDtypeStruct((part, width), bf16),) * CHUNKS
        + (
            jax.ShapeDtypeStruct((2, 3 * entries, part, LANES), f32),
            jax.ShapeDtypeStruct((2, part, coeffs), f32),
            jax.ShapeDtypeStruct((2, part, coeffs), f32),
            jax.ShapeDtypeStruct(weights.shape, bf16),
        ),
        in_specs=[VMEM] * 3,
        out_specs=(VMEM,) * (4 + CHUNKS),
        scratch_shapes=[pltpu.SemaphoreType.DMA],
        input_output_aliases={2: 3 + CHUNKS},
        compiler_params=LIMIT,
        name="unpack",
    )(received, other, weights)

    kept = jnp.zeros((columns, 2, own_windows * ROWS, width), bf16)
    for turn in range(chips):
        for c in range(CHUNKS):
            chunks[c], kept = stage(turn, c, entries, coeffs, chunks[c], weights, mixing, cs, ds, kept)
            if turn + 1 < chips:
                chunks[c] = lax.ppermute(chunks[c], "sec", [(2 * turn + k, 2 * turn + 2 + k) for k in range(2)])

    kept = kept.reshape(members, own_windows * ROWS, width)
    got = lax.all_to_all(kept, ("win", "sec"), 0, 0, axis_index_groups=groups, tiled=True)
    return pl.pallas_call(
        repack_kernel,
        out_shape=jax.ShapeDtypeStruct(initial.shape, bf16),
        in_specs=[VMEM],
        out_specs=VMEM,
        compiler_params=LIMIT,
        name="repack",
    )(got)[None]


def solution(mesh):
    placed = (
        P(None, "win", None, None),
        P("sec", None, None, None, None),
        P("sec", "win", None),
        P("sec", "win", None),
        P("sec", "win", None),
        P("sec", "win"),
    )
    return jax.shard_map(
        local,
        mesh=mesh,
        in_specs=placed,
        out_specs=P("sec", None, "win", None, None),
        check_vma=False,
    )
```

time: 149 us -> 128 us (0.86)
  waiting for transfers between devices: 80.6 us -> 51.1 us
  starting transfers between devices: 11.3 us -> 21.9 us
  local copies, waits for them, and re-layouts: 5.97 us -> 0.02 us
  Pallas kernels: 4.04 us -> 7.41 us
    ppermute x15 -> x30, waiting for transfers between devices: 80.6 us -> 51.1 us  [local(): lax.ppermute(chunks[c], 'sec', [(2 * turn + k, 2 * turn + 2 + k) for k in...]
    ppermute x15 -> x30, starting transfers between devices: 10.7 us -> 21.2 us  [local(): lax.ppermute(chunks[c], 'sec', [(2 * turn + k, 2 * turn + 2 + k) for k in...]
    unnamed x12 -> x0, local copies, waits for them, and re-layouts: 5.22 us -> none
    pallas_call x19 -> x35, Pallas kernels: 4.04 us -> 7.41 us  [the longest x32 3.96 us: stage(): pl.pallas_call(body, out_shape=(jax.ShapeDtypeStruct(field.shape, field.d...]
  transfers between devices with their start and end apart: 16 -> 31, of which waited for: 1 -> 2; matrix products, arithmetic and copies ran while one was open for 0% -> 0% of each run, Pallas kernels for 1% -> 3%
where the time goes in v2:
time: 128 us; the launch traced here: 127 us
  waiting for transfers between devices  51.1 us (40%)
  blocking collectives  46.2 us (36%)
  starting transfers between devices  21.9 us (17%)
  Pallas kernels  7.41 us (6%)
    ppermute x30, waiting for transfers between devices, local(): lax.ppermute(chunks[c], 'sec', [(2 * turn + k, 2 * turn + 2 + k) for k in...  51.1 us
    all_to_all x1, blocking collectives, local(): lax.all_to_all(kept, ('win', 'sec'), 0, 0, axis_index_groups=groups, tile...  26.1 us
    ppermute x30, starting transfers between devices, local(): lax.ppermute(chunks[c], 'sec', [(2 * turn + k, 2 * turn + 2 + k) for k in...  21.2 us
    all_to_all x1, blocking collectives, local(): lax.all_to_all(payload, ('win', 'sec'), 0, 0, axis_index_groups=groups, t...  20.1 us
    pallas_call x32, Pallas kernels, stage(): pl.pallas_call(body, out_shape=(jax.ShapeDtypeStruct(field.shape, field.d...  3.96 us
  transfers between devices with their start and end apart: 31, of which 2 were waited for; matrix products, arithmetic and copies ran while one was open for 0% of the time, Pallas kernels for 3%

profile of v2, /device:TPU:31, one launch (start us, length us, event | category | flops | bytes accessed | tf_op | source)
XLA Modules:
  0.0 127.4 jit_solution(11689627360853437500)
XLA Ops:
  0.0 0.7 collective-permute-start
  0.7 1.8 %pack.1 = (bf16[16,16,512]{2,1,0:T(8,128)(2,1)S(1)}, bf16[2,4096,256]{2,1,0:T(8,128)(2,1)S(1)}) custom-call(bf16[5,2,24,512]{3,2,1,0:T(8,128)(2,1)} %initial_hbm.1, f32[1,2,256]{2,1,0:T(2,128)} %screen_hbm.1, s32[1,2,6]{2,1,0:T(2,128)} %links_hbm.1, s32[1,2,6]{2,1,0:T(2,128)} %kinds_hbm.1, s32[1,2]{1,0:T(1,128)} %counts_hbm.1, bf16[4096,256]{1,0:T(8,128)(2,1)} %bitcast.5), custom_call_target="tpu_custom_call" | custom-call | tf_op jit(solution)/shard_map/pack/pallas_call | solution.py:195
  2.5 20.1 %all_to_all.10.received_ref = bf16[16,16,512]{2,1,0:T(8,128)(2,1)S(1)} all-to-all(bf16[16,16,512]{2,1,0:T(8,128)(2,1)S(1)} %get-tuple-element.75), channel_id=1, replica_groups={{0,1,32,33,64,65,96,97,128,129,160,161,192,193,224,225},{2,3,34,35,66,6..., dimensions={0} | all-to-all | bytes 524288 | tf_op jit(solution)/shard_map/all_to_all | solution.py:214
  22.6 0.9 unpack.1
  23.5 0.7 collective-permute-start.2
  24.2 0.7 collective-permute-start.1
  25.7 0.7 collective-permute-start.3
  26.4 0.7 collective-permute-start.6
  27.1 0.7 collective-permute-start.5
  27.8 0.7 collective-permute-start.8
  28.5 0.7 collective-permute-start.7
  29.2 0.7 collective-permute-start.10
  29.9 0.7 collective-permute-start.9
  30.7 0.7 collective-permute-start.12
  31.4 0.7 collective-permute-start.11
  32.1 0.7 collective-permute-start.14
  33.5 0.7 collective-permute-start.16
  34.2 0.7 collective-permute-start.15
  34.9 0.7 collective-permute-start.18
  36.4 0.7 collective-permute-start.20
  37.1 0.7 collective-permute-start.19
  37.8 0.7 collective-permute-start.22
  39.4 0.7 collective-permute-start.24
  40.1 0.7 collective-permute-start.23
  43.7 1.3 %collective-permute-start.30 = (bf16[64,512]{1,0:T(8,128)(2,1)S(1)}, bf16[64,512]{1,0:T(8,128)(2,1)S(1)}, u32[]{:S(2)}, u32[]{:S(2)}) collective-permute-start(bf16[64,512]{1,0:T(8,128)(2,1)S(1)} %get-tuple-element.141), channel_id=1, source_target_pairs={{28,30},{29,31},{60,62},{61,63},{92,94},{93,95},{124,126},{125,127... | collective-permute-start | bytes 196616 | tf_op jit(solution)/shard_map/ppermute | solution.py:242
  45.0 1.3 %collective-permute-start.29 = (bf16[64,512]{1,0:T(8,128)(2,1)S(1)}, bf16[64,512]{1,0:T(8,128)(2,1)S(1)}, u32[]{:S(2)}, u32[]{:S(2)}) collective-permute-start(bf16[64,512]{1,0:T(8,128)(2,1)S(1)} %get-tuple-element.140), channel_id=1, source_target_pairs={{28,30},{29,31},{60,62},{61,63},{92,94},{93,95},{124,126},{125,127... | collective-permute-start | bytes 196616 | tf_op jit(solution)/shard_map/ppermute | solution.py:242
  46.3 49.4 %collective-permute-done.30.x_ref = bf16[64,512]{1,0:T(8,128)(2,1)S(1)} collective-permute-done((bf16[64,512]{1,0:T(8,128)(2,1)S(1)}, bf16[64,512]{1,0:T(8,128)(2,1)S(1)}, u32[]{:S(2)}, u32[]{:S(2)}) %collective-permute-start.30) | collective-permute-done | bytes 65568 | tf_op jit(solution)/shard_map/ppermute | solution.py:242
  95.7 1.6 %stage.62 = (bf16[64,512]{1,0:T(8,128)(2,1)}, bf16[8,2,16,512]{3,2,1,0:T(8,128)(2,1)S(1)}) custom-call(bf16[64,512]{1,0:T(8,128)(2,1)S(1)} %collective-permute-done.30.x_ref, bf16[2,4096,256]{2,1,0:T(8,128)(2,1)S(1)} %get-tuple-element.78.w_ref, f32[2,24,64,128]{3,2,1,0:T(8,128)S(1)} %get-tuple-element.79.mix_ref, ...), custom_call_target="tpu_custom_call", output_to_operand_aliasing={{1}: (5, {})} | custom-call | flops 536870912 | bytes 4194304 | tf_op jit(solution)/shard_map/stage/pallas_call | solution.py:164
  97.3 1.6 %collective-permute-done.29.x_ref = bf16[64,512]{1,0:T(8,128)(2,1)S(1)} collective-permute-done((bf16[64,512]{1,0:T(8,128)(2,1)S(1)}, bf16[64,512]{1,0:T(8,128)(2,1)S(1)}, u32[]{:S(2)}, u32[]{:S(2)}) %collective-permute-start.29) | collective-permute-done | bytes 65568 | tf_op jit(solution)/shard_map/ppermute | solution.py:242
  98.9 1.6 %stage.63 = (bf16[64,512]{1,0:T(8,128)(2,1)}, bf16[8,2,16,512]{3,2,1,0:T(8,128)(2,1)S(1)}) custom-call(bf16[64,512]{1,0:T(8,128)(2,1)S(1)} %collective-permute-done.29.x_ref, bf16[2,4096,256]{2,1,0:T(8,128)(2,1)S(1)} %get-tuple-element.78.w_ref, f32[2,24,64,128]{3,2,1,0:T(8,128)S(1)} %get-tuple-element.79.mix_ref, ...), custom_call_target="tpu_custom_call", output_to_operand_aliasing={{1}: (5, {})} | custom-call | flops 536870912 | bytes 4194304 | tf_op jit(solution)/shard_map/stage/pallas_call | solution.py:164
  100.5 26.1 %all_to_all.11.got_ref = bf16[16,16,512]{2,1,0:T(8,128)(2,1)S(1)} all-to-all(bf16[16,16,512]{2,1,0:T(8,128)(2,1)S(1)} %bitcast.3), channel_id=1, replica_groups={{0,1,32,33,64,65,96,97,128,129,160,161,192,193,224,225},{2,3,34,35,66,6..., dimensions={0} | all-to-all | bytes 524288 | tf_op jit(solution)/shard_map/all_to_all | solution.py:245
  126.6 0.8 repack.1
  (68 shorter events, 6.2 us)
Async XLA Ops:
  0.0 22.6 %collective-permute-start = (bf16[4096,256]{1,0:T(8,128)(2,1)}, bf16[4096,256]{1,0:T(8,128)(2,1)S(1)}, u32[]{:S(2)}, u32[]{:S(2)}) collective-permute-start(bf16[4096,256]{1,0:T(8,128)(2,1)} %bitcast.4), channel_id=1, source_target_pairs={{0,1},{1,0},{2,3},{3,2},{4,5},{5,4},{6,7},{7,6},{8,9},{9,8},{10,11... | collective-permute-start | bytes 6291464 | tf_op jit(solution)/shard_map/ppermute | solution.py:193
  23.5 1.4 %collective-permute-start.2 = (bf16[64,512]{1,0:T(8,128)(2,1)S(1)}, bf16[64,512]{1,0:T(8,128)(2,1)S(1)}, u32[]{:S(2)}, u32[]{:S(2)}) collective-permute-start(bf16[64,512]{1,0:T(8,128)(2,1)S(1)} %get-tuple-element.85), channel_id=1, source_target_pairs={{0,2},{1,3},{32,34},{33,35},{64,66},{65,67},{96,98},{97,99},{128,1... | collective-permute-start | bytes 196616 | tf_op jit(solution)/shard_map/ppermute | solution.py:242
  24.2 1.4 %collective-permute-start.1 = (bf16[64,512]{1,0:T(8,128)(2,1)S(1)}, bf16[64,512]{1,0:T(8,128)(2,1)S(1)}, u32[]{:S(2)}, u32[]{:S(2)}) collective-permute-start(bf16[64,512]{1,0:T(8,128)(2,1)S(1)} %get-tuple-element.84), channel_id=1, source_target_pairs={{0,2},{1,3},{32,34},{33,35},{64,66},{65,67},{96,98},{97,99},{128,1... | collective-permute-start | bytes 196616 | tf_op jit(solution)/shard_map/ppermute | solution.py:242
  25.0 1.4 %collective-permute-start.4 = (bf16[64,512]{1,0:T(8,128)(2,1)S(1)}, bf16[64,512]{1,0:T(8,128)(2,1)S(1)}, u32[]{:S(2)}, u32[]{:S(2)}) collective-permute-start(bf16[64,512]{1,0:T(8,128)(2,1)S(1)} %get-tuple-element.89), channel_id=1, source_target_pairs={{2,4},{3,5},{34,36},{35,37},{66,68},{67,69},{98,100},{99,101},{130... | collective-permute-start | bytes 196616 | tf_op jit(solution)/shard_map/ppermute | solution.py:242
  25.7 1.4 %collective-permute-start.3 = (bf16[64,512]{1,0:T(8,128)(2,1)S(1)}, bf16[64,512]{1,0:T(8,128)(2,1)S(1)}, u32[]{:S(2)}, u32[]{:S(2)}) collective-permute-start(bf16[64,512]{1,0:T(8,128)(2,1)S(1)} %get-tuple-element.88), channel_id=1, source_target_pairs={{2,4},{3,5},{34,36},{35,37},{66,68},{67,69},{98,100},{99,101},{130... | collective-permute-start | bytes 196616 | tf_op jit(solution)/shard_map/ppermute | solution.py:242
  26.4 1.4 %collective-permute-start.6 = (bf16[64,512]{1,0:T(8,128)(2,1)S(1)}, bf16[64,512]{1,0:T(8,128)(2,1)S(1)}, u32[]{:S(2)}, u32[]{:S(2)}) collective-permute-start(bf16[64,512]{1,0:T(8,128)(2,1)S(1)} %get-tuple-element.93), channel_id=1, source_target_pairs={{4,6},{5,7},{36,38},{37,39},{68,70},{69,71},{100,102},{101,103},{1... | collective-permute-start | bytes 196616 | tf_op jit(solution)/shard_map/ppermute | solution.py:242
  27.1 1.4 %collective-permute-start.5 = (bf16[64,512]{1,0:T(8,128)(2,1)S(1)}, bf16[64,512]{1,0:T(8,128)(2,1)S(1)}, u32[]{:S(2)}, u32[]{:S(2)}) collective-permute-start(bf16[64,512]{1,0:T(8,128)(2,1)S(1)} %get-tuple-element.92), channel_id=1, source_target_pairs={{4,6},{5,7},{36,38},{37,39},{68,70},{69,71},{100,102},{101,103},{1... | collective-permute-start | bytes 196616 | tf_op jit(solution)/shard_map/ppermute | solution.py:242
  27.8 1.4 %collective-permute-start.8 = (bf16[64,512]{1,0:T(8,128)(2,1)S(1)}, bf16[64,512]{1,0:T(8,128)(2,1)S(1)}, u32[]{:S(2)}, u32[]{:S(2)}) collective-permute-start(bf16[64,512]{1,0:T(8,128)(2,1)S(1)} %get-tuple-element.97), channel_id=1, source_target_pairs={{6,8},{7,9},{38,40},{39,41},{70,72},{71,73},{102,104},{103,105},{1... | collective-permute-start | bytes 196616 | tf_op jit(solution)/shard_map/ppermute | solution.py:242
  28.5 1.4 %collective-permute-start.7 = (bf16[64,512]{1,0:T(8,128)(2,1)S(1)}, bf16[64,512]{1,0:T(8,128)(2,1)S(1)}, u32[]{:S(2)}, u32[]{:S(2)}) collective-permute-start(bf16[64,512]{1,0:T(8,128)(2,1)S(1)} %get-tuple-element.96), channel_id=1, source_target_pairs={{6,8},{7,9},{38,40},{39,41},{70,72},{71,73},{102,104},{103,105},{1... | collective-permute-start | bytes 196616 | tf_op jit(solution)/shard_map/ppermute | solution.py:242
  29.2 1.4 %collective-permute-start.10 = (bf16[64,512]{1,0:T(8,128)(2,1)S(1)}, bf16[64,512]{1,0:T(8,128)(2,1)S(1)}, u32[]{:S(2)}, u32[]{:S(2)}) collective-permute-start(bf16[64,512]{1,0:T(8,128)(2,1)S(1)} %get-tuple-element.101), channel_id=1, source_target_pairs={{8,10},{9,11},{40,42},{41,43},{72,74},{73,75},{104,106},{105,107},... | collective-permute-start | bytes 196616 | tf_op jit(solution)/shard_map/ppermute | solution.py:242
  29.9 1.4 %collective-permute-start.9 = (bf16[64,512]{1,0:T(8,128)(2,1)S(1)}, bf16[64,512]{1,0:T(8,128)(2,1)S(1)}, u32[]{:S(2)}, u32[]{:S(2)}) collective-permute-start(bf16[64,512]{1,0:T(8,128)(2,1)S(1)} %get-tuple-element.100), channel_id=1, source_target_pairs={{8,10},{9,11},{40,42},{41,43},{72,74},{73,75},{104,106},{105,107},... | collective-permute-start | bytes 196616 | tf_op jit(solution)/shard_map/ppermute | solution.py:242
  30.7 1.4 %collective-permute-start.12 = (bf16[64,512]{1,0:T(8,128)(2,1)S(1)}, bf16[64,512]{1,0:T(8,128)(2,1)S(1)}, u32[]{:S(2)}, u32[]{:S(2)}) collective-permute-start(bf16[64,512]{1,0:T(8,128)(2,1)S(1)} %get-tuple-element.105), channel_id=1, source_target_pairs={{10,12},{11,13},{42,44},{43,45},{74,76},{75,77},{106,108},{107,109... | collective-permute-start | bytes 196616 | tf_op jit(solution)/shard_map/ppermute | solution.py:242
  31.4 1.4 %collective-permute-start.11 = (bf16[64,512]{1,0:T(8,128)(2,1)S(1)}, bf16[64,512]{1,0:T(8,128)(2,1)S(1)}, u32[]{:S(2)}, u32[]{:S(2)}) collective-permute-start(bf16[64,512]{1,0:T(8,128)(2,1)S(1)} %get-tuple-element.104), channel_id=1, source_target_pairs={{10,12},{11,13},{42,44},{43,45},{74,76},{75,77},{106,108},{107,109... | collective-permute-start | bytes 196616 | tf_op jit(solution)/shard_map/ppermute | solution.py:242
  32.1 1.4 %collective-permute-start.14 = (bf16[64,512]{1,0:T(8,128)(2,1)S(1)}, bf16[64,512]{1,0:T(8,128)(2,1)S(1)}, u32[]{:S(2)}, u32[]{:S(2)}) collective-permute-start(bf16[64,512]{1,0:T(8,128)(2,1)S(1)} %get-tuple-element.109), channel_id=1, source_target_pairs={{12,14},{13,15},{44,46},{45,47},{76,78},{77,79},{108,110},{109,111... | collective-permute-start | bytes 196616 | tf_op jit(solution)/shard_map/ppermute | solution.py:242
  32.8 1.4 %collective-permute-start.13 = (bf16[64,512]{1,0:T(8,128)(2,1)S(1)}, bf16[64,512]{1,0:T(8,128)(2,1)S(1)}, u32[]{:S(2)}, u32[]{:S(2)}) collective-permute-start(bf16[64,512]{1,0:T(8,128)(2,1)S(1)} %get-tuple-element.108), channel_id=1, source_target_pairs={{12,14},{13,15},{44,46},{45,47},{76,78},{77,79},{108,110},{109,111... | collective-permute-start | bytes 196616 | tf_op jit(solution)/shard_map/ppermute | solution.py:242
  33.5 1.4 %collective-permute-start.16 = (bf16[64,512]{1,0:T(8,128)(2,1)S(1)}, bf16[64,512]{1,0:T(8,128)(2,1)S(1)}, u32[]{:S(2)}, u32[]{:S(2)}) collective-permute-start(bf16[64,512]{1,0:T(8,128)(2,1)S(1)} %get-tuple-element.113), channel_id=1, source_target_pairs={{14,16},{15,17},{46,48},{47,49},{78,80},{79,81},{110,112},{111,113... | collective-permute-start | bytes 196616 | tf_op jit(solution)/shard_map/ppermute | solution.py:242
  34.2 1.4 %collective-permute-start.15 = (bf16[64,512]{1,0:T(8,128)(2,1)S(1)}, bf16[64,512]{1,0:T(8,128)(2,1)S(1)}, u32[]{:S(2)}, u32[]{:S(2)}) collective-permute-start(bf16[64,512]{1,0:T(8,128)(2,1)S(1)} %get-tuple-element.112), channel_id=1, source_target_pairs={{14,16},{15,17},{46,48},{47,49},{78,80},{79,81},{110,112},{111,113... | collective-permute-start | bytes 196616 | tf_op jit(solution)/shard_map/ppermute | solution.py:242
  34.9 1.4 %collective-permute-start.18 = (bf16[64,512]{1,0:T(8,128)(2,1)S(1)}, bf16[64,512]{1,0:T(8,128)(2,1)S(1)}, u32[]{:S(2)}, u32[]{:S(2)}) collective-permute-start(bf16[64,512]{1,0:T(8,128)(2,1)S(1)} %get-tuple-element.117), channel_id=1, source_target_pairs={{16,18},{17,19},{48,50},{49,51},{80,82},{81,83},{112,114},{113,115... | collective-permute-start | bytes 196616 | tf_op jit(solution)/shard_map/ppermute | solution.py:242
  35.6 1.4 %collective-permute-start.17 = (bf16[64,512]{1,0:T(8,128)(2,1)S(1)}, bf16[64,512]{1,0:T(8,128)(2,1)S(1)}, u32[]{:S(2)}, u32[]{:S(2)}) collective-permute-start(bf16[64,512]{1,0:T(8,128)(2,1)S(1)} %get-tuple-element.116), channel_id=1, source_target_pairs={{16,18},{17,19},{48,50},{49,51},{80,82},{81,83},{112,114},{113,115... | collective-permute-start | bytes 196616 | tf_op jit(solution)/shard_map/ppermute | solution.py:242
  36.4 1.4 %collective-permute-start.20 = (bf16[64,512]{1,0:T(8,128)(2,1)S(1)}, bf16[64,512]{1,0:T(8,128)(2,1)S(1)}, u32[]{:S(2)}, u32[]{:S(2)}) collective-permute-start(bf16[64,512]{1,0:T(8,128)(2,1)S(1)} %get-tuple-element.121), channel_id=1, source_target_pairs={{18,20},{19,21},{50,52},{51,53},{82,84},{83,85},{114,116},{115,117... | collective-permute-start | bytes 196616 | tf_op jit(solution)/shard_map/ppermute | solution.py:242
  37.1 1.4 %collective-permute-start.19 = (bf16[64,512]{1,0:T(8,128)(2,1)S(1)}, bf16[64,512]{1,0:T(8,128)(2,1)S(1)}, u32[]{:S(2)}, u32[]{:S(2)}) collective-permute-start(bf16[64,512]{1,0:T(8,128)(2,1)S(1)} %get-tuple-element.120), channel_id=1, source_target_pairs={{18,20},{19,21},{50,52},{51,53},{82,84},{83,85},{114,116},{115,117... | collective-permute-start | bytes 196616 | tf_op jit(solution)/shard_map/ppermute | solution.py:242
  37.8 1.4 %collective-permute-start.22 = (bf16[64,512]{1,0:T(8,128)(2,1)S(1)}, bf16[64,512]{1,0:T(8,128)(2,1)S(1)}, u32[]{:S(2)}, u32[]{:S(2)}) collective-permute-start(bf16[64,512]{1,0:T(8,128)(2,1)S(1)} %get-tuple-element.125), channel_id=1, source_target_pairs={{20,22},{21,23},{52,54},{53,55},{84,86},{85,87},{116,118},{117,119... | collective-permute-start | bytes 196616 | tf_op jit(solution)/shard_map/ppermute | solution.py:242
  38.5 1.6 %collective-permute-start.21 = (bf16[64,512]{1,0:T(8,128)(2,1)S(1)}, bf16[64,512]{1,0:T(8,128)(2,1)S(1)}, u32[]{:S(2)}, u32[]{:S(2)}) collective-permute-start(bf16[64,512]{1,0:T(8,128)(2,1)S(1)} %get-tuple-element.124), channel_id=1, source_target_pairs={{20,22},{21,23},{52,54},{53,55},{84,86},{85,87},{116,118},{117,119... | collective-permute-start | bytes 196616 | tf_op jit(solution)/shard_map/ppermute | solution.py:242
  39.4 1.4 %collective-permute-start.24 = (bf16[64,512]{1,0:T(8,128)(2,1)S(1)}, bf16[64,512]{1,0:T(8,128)(2,1)S(1)}, u32[]{:S(2)}, u32[]{:S(2)}) collective-permute-start(bf16[64,512]{1,0:T(8,128)(2,1)S(1)} %get-tuple-element.129), channel_id=1, source_target_pairs={{22,24},{23,25},{54,56},{55,57},{86,88},{87,89},{118,120},{119,121... | collective-permute-start | bytes 196616 | tf_op jit(solution)/shard_map/ppermute | solution.py:242
  40.1 1.4 %collective-permute-start.23 = (bf16[64,512]{1,0:T(8,128)(2,1)S(1)}, bf16[64,512]{1,0:T(8,128)(2,1)S(1)}, u32[]{:S(2)}, u32[]{:S(2)}) collective-permute-start(bf16[64,512]{1,0:T(8,128)(2,1)S(1)} %get-tuple-element.128), channel_id=1, source_target_pairs={{22,24},{23,25},{54,56},{55,57},{86,88},{87,89},{118,120},{119,121... | collective-permute-start | bytes 196616 | tf_op jit(solution)/shard_map/ppermute | solution.py:242
  40.8 1.4 %collective-permute-start.26 = (bf16[64,512]{1,0:T(8,128)(2,1)S(1)}, bf16[64,512]{1,0:T(8,128)(2,1)S(1)}, u32[]{:S(2)}, u32[]{:S(2)}) collective-permute-start(bf16[64,512]{1,0:T(8,128)(2,1)S(1)} %get-tuple-element.133), channel_id=1, source_target_pairs={{24,26},{25,27},{56,58},{57,59},{88,90},{89,91},{120,122},{121,123... | collective-permute-start | bytes 196616 | tf_op jit(solution)/shard_map/ppermute | solution.py:242
  41.5 1.4 %collective-permute-start.25 = (bf16[64,512]{1,0:T(8,128)(2,1)S(1)}, bf16[64,512]{1,0:T(8,128)(2,1)S(1)}, u32[]{:S(2)}, u32[]{:S(2)}) collective-permute-start(bf16[64,512]{1,0:T(8,128)(2,1)S(1)} %get-tuple-element.132), channel_id=1, source_target_pairs={{24,26},{25,27},{56,58},{57,59},{88,90},{89,91},{120,122},{121,123... | collective-permute-start | bytes 196616 | tf_op jit(solution)/shard_map/ppermute | solution.py:242
  42.2 1.4 %collective-permute-start.28 = (bf16[64,512]{1,0:T(8,128)(2,1)S(1)}, bf16[64,512]{1,0:T(8,128)(2,1)S(1)}, u32[]{:S(2)}, u32[]{:S(2)}) collective-permute-start(bf16[64,512]{1,0:T(8,128)(2,1)S(1)} %get-tuple-element.137), channel_id=1, source_target_pairs={{26,28},{27,29},{58,60},{59,61},{90,92},{91,93},{122,124},{123,125... | collective-permute-start | bytes 196616 | tf_op jit(solution)/shard_map/ppermute | solution.py:242
  42.9 2.0 %collective-permute-start.27 = (bf16[64,512]{1,0:T(8,128)(2,1)S(1)}, bf16[64,512]{1,0:T(8,128)(2,1)S(1)}, u32[]{:S(2)}, u32[]{:S(2)}) collective-permute-start(bf16[64,512]{1,0:T(8,128)(2,1)S(1)} %get-tuple-element.136), channel_id=1, source_target_pairs={{26,28},{27,29},{58,60},{59,61},{90,92},{91,93},{122,124},{123,125... | collective-permute-start | bytes 196616 | tf_op jit(solution)/shard_map/ppermute | solution.py:242
  43.7 52.1 %collective-permute-start.30 = (bf16[64,512]{1,0:T(8,128)(2,1)S(1)}, bf16[64,512]{1,0:T(8,128)(2,1)S(1)}, u32[]{:S(2)}, u32[]{:S(2)}) collective-permute-start(bf16[64,512]{1,0:T(8,128)(2,1)S(1)} %get-tuple-element.141), channel_id=1, source_target_pairs={{28,30},{29,31},{60,62},{61,63},{92,94},{93,95},{124,126},{125,127... | collective-permute-start | bytes 196616 | tf_op jit(solution)/shard_map/ppermute | solution.py:242
  45.0 53.9 %collective-permute-start.29 = (bf16[64,512]{1,0:T(8,128)(2,1)S(1)}, bf16[64,512]{1,0:T(8,128)(2,1)S(1)}, u32[]{:S(2)}, u32[]{:S(2)}) collective-permute-start(bf16[64,512]{1,0:T(8,128)(2,1)S(1)} %get-tuple-element.140), channel_id=1, source_target_pairs={{28,30},{29,31},{60,62},{61,63},{92,94},{93,95},{124,126},{125,127... | collective-permute-start | bytes 196616 | tf_op jit(solution)/shard_map/ppermute | solution.py:242

commit v3 on v2

--- a/solution.py
+++ b/solution.py
@@ -11,6 +11,7 @@
 LANES = 128
 CHUNKS = 2
 UNITS = 2
+FIRST_PAIR = 8
 VMEM = pl.BlockSpec(memory_space=pltpu.VMEM)
 HBM = pl.BlockSpec(memory_space=pltpu.HBM)
 LIMIT = pltpu.CompilerParams(vmem_limit_bytes=16 << 20)
@@ -70,12 +71,15 @@
     copies[-1].wait()
 
 
-def unpack_kernel(entries, coeffs, received_ref, other_ref, field_refs, mix_ref, cs_ref, ds_ref, weights_ref, sem):
-    copy = pltpu.make_async_copy(other_ref, weights_ref.at[1 - lax.axis_index("sec") % 2], sem)
-    copy.start()
+def unpack_kernel(entries, coeffs, received_ref, tables_at, placed, field_refs, mix_ref, cs_ref, ds_ref, weights_ref, sems):
+    copies = [
+        pltpu.make_async_copy(source, weights_ref.at[slot], sems.at[i]) for i, (source, slot) in enumerate(placed)
+    ]
+    for copy in copies:
+        copy.start()
+    part = ROWS // CHUNKS
     columns = received_ref.shape[0] // 2
     own_windows = 2
-    part = ROWS // len(field_refs)
     for z in range(columns):
         blocks = [received_ref[2 * z + core].astype(jnp.float32) for core in range(2)]
         at = pl.ds(own_windows * part * z, own_windows * part)
@@ -85,10 +89,10 @@
         for core in range(2):
             trigs, hits = [], []
             for w in range(own_windows):
-                row = ROWS + 2 * w
+                row = tables_at + 2 * w
                 trig = blocks[core][row : row + 1] + blocks[core][row + 1 : row + 2]
                 trigs.append(jnp.broadcast_to(trig, (part, 2 * coeffs)))
-                row = ROWS + 2 * own_windows + w
+                row = tables_at + 2 * own_windows + w
                 hits.append(jnp.broadcast_to(blocks[core][row : row + 1, :LANES], (part, LANES)))
             trig = jnp.concatenate(trigs, axis=0)
             cs_ref[core, at, :] = trig[:, :coeffs]
@@ -96,7 +100,8 @@
             hit = jnp.concatenate(hits, axis=0)
             for spot in range(3 * entries):
                 mix_ref[core, spot, at, :] = jnp.broadcast_to(hit[:, spot : spot + 1], (own_windows * part, LANES))
-    copy.wait()
+    for copy in copies:
+        copy.wait()
 
 
 def repack_kernel(got_ref, out_ref):
@@ -151,26 +156,30 @@
         lax.fori_loop(0, sections, one, 0)
 
 
-def stage(turn, chunk, entries, coeffs, field, weights, mixing, cs, ds, kept):
+def stage(turn, chunk, entries, coeffs, last, field, weights, mixing, cs, ds, kept):
     flops = 16 * entries * field.shape[0] * coeffs * coeffs
 
-    def body(x_ref, w_ref, mix_ref, cs_ref, ds_ref, kept_ref, y_ref, out_ref):
+    def body(x_ref, w_ref, mix_ref, cs_ref, ds_ref, kept_ref, *outs):
+        out_ref, y_ref = outs if last else outs[::-1]
         sums = [pltpu.ACC(unit)((field.shape[0], coeffs), jnp.float32) for unit in range(UNITS) for _ in range(2)]
         run = functools.partial(
             stage_kernel, turn, chunk, entries, coeffs, x_ref, w_ref, mix_ref, cs_ref, ds_ref, y_ref, out_ref
         )
         pl.run_scoped(run, *sums)
 
-    return pl.pallas_call(
+    sent = jax.ShapeDtypeStruct(field.shape, field.dtype)
+    results = pl.pallas_call(
         body,
-        out_shape=(jax.ShapeDtypeStruct(field.shape, field.dtype), jax.ShapeDtypeStruct(kept.shape, kept.dtype)),
+        out_shape=((() if last else (sent,)) + (jax.ShapeDtypeStruct(kept.shape, kept.dtype),)),
         in_specs=[VMEM] * 6,
-        out_specs=(VMEM, VMEM),
-        input_output_aliases={5: 1},
+        out_specs=(VMEM,) * (1 if last else 2),
+        scratch_shapes=[pltpu.VMEM(field.shape, field.dtype)] if last else [],
+        input_output_aliases={5: 0 if last else 1},
         cost_estimate=pl.CostEstimate(flops=flops, bytes_accessed=weights.size * 2, transcendentals=0),
         compiler_params=LIMIT,
         name="stage",
     )(field, weights, mixing, cs, ds, kept)
+    return (None, results[0]) if last else results
 
 
 def local(initial, props, screen, links, kinds, counts):
@@ -191,6 +200,10 @@
 
     own = props.reshape(entries * 2 * coeffs, coeffs)
     other = lax.ppermute(own, "sec", [(s, s ^ 1) for s in range(sections)])
+    lend = [(c if c % 4 == 2 else c + 1, c + 1 if c % 4 == 2 else c) for c in range(FIRST_PAIR, chips - 2, 2)]
+    takers, givers = [t for t, _ in lend], [g for _, g in lend]
+    to_taker = [(2 * g + k, 2 * t + k) for t, g in lend for k in range(2)]
+    lent = lax.ppermute(own, "sec", to_taker)
 
     payload, weights = pl.pallas_call(
         functools.partial(pack_kernel, entries),
@@ -213,33 +226,81 @@
     )(*[pltpu.with_memory_space_constraint(a, pltpu.HBM) for a in (initial, screen, links, kinds, counts, own)])
     received = lax.all_to_all(payload, ("win", "sec"), 0, 0, axis_index_groups=groups, tiled=True)
     part = points // CHUNKS
+    tables = (
+        jax.ShapeDtypeStruct((2, 3 * entries, part, LANES), f32),
+        jax.ShapeDtypeStruct((2, part, coeffs), f32),
+        jax.ShapeDtypeStruct((2, part, coeffs), f32),
+        jax.ShapeDtypeStruct(weights.shape, bf16),
+    )
 
     def unpack(received_ref, other_ref, weights_in_ref, *refs):
-        unpack_kernel(entries, coeffs, received_ref, other_ref, refs[:CHUNKS], *refs[CHUNKS:])
-
-    *chunks, mixing, cs, ds, weights = pl.pallas_call(
+        placed = [(other_ref, 1 - lax.axis_index("sec") % 2)]
+        for member in range(members):
+            refs[-2][member] = received_ref[member, ROWS:]
+        unpack_kernel(entries, coeffs, received_ref, ROWS, placed, refs[:CHUNKS], *refs[CHUNKS:-2], refs[-1])
+
+    *chunks, mixing, cs, ds, weights, lent_tables = pl.pallas_call(
         unpack,
         out_shape=(jax.ShapeDtypeStruct((part, width), bf16),) * CHUNKS
-        + (
-            jax.ShapeDtypeStruct((2, 3 * entries, part, LANES), f32),
-            jax.ShapeDtypeStruct((2, part, coeffs), f32),
-            jax.ShapeDtypeStruct((2, part, coeffs), f32),
-            jax.ShapeDtypeStruct(weights.shape, bf16),
-        ),
+        + tables
+        + (jax.ShapeDtypeStruct((members, ROWS, width), bf16),),
         in_specs=[VMEM] * 3,
-        out_specs=(VMEM,) * (4 + CHUNKS),
-        scratch_shapes=[pltpu.SemaphoreType.DMA],
+        out_specs=(VMEM,) * (5 + CHUNKS),
+        scratch_shapes=[pltpu.SemaphoreType.DMA((1,))],
         input_output_aliases={2: 3 + CHUNKS},
         compiler_params=LIMIT,
         name="unpack",
     )(received, other, weights)
 
-    kept = jnp.zeros((columns, 2, own_windows * ROWS, width), bf16)
-    for turn in range(chips):
+    lent_tables = lax.ppermute(lent_tables, "sec", to_taker)
+
+    def among(chip, chosen):
+        return functools.reduce(jnp.logical_or, [chip == c for c in chosen])
+
+    def unpack_lent(received_ref, near_ref, far_ref, *refs):
+        core = lax.axis_index("sec") % 2
+
+        @pl.when(among(lax.axis_index("sec") // 2, takers))
+        def _():
+            unpack_kernel(entries, coeffs, received_ref, 0, [(near_ref, core), (far_ref, 1 - core)], (), *refs)
+
+    plan = [(c, "own") for c in range(FIRST_PAIR)]
+    for t, g in lend:
+        plan += [(t, "own"), (t, "lent")] if t < g else [(t, "lent"), (t, "own")]
+    plan += [(c, "own") for c in range(chips - 2, chips)]
+    stops = [[plan[0][0], []]]
+    for c, kind in plan:
+        if stops[-1][0] != c:
+            stops.append([c, []])
+        stops[-1][1].append(kind)
+
+    kept = {kind: jnp.zeros((columns, 2, own_windows * ROWS, width), bf16) for kind in ("own", "lent")}
+    lent_tables, near, weights = lax.optimization_barrier((lent_tables, lent, weights))
+    sets = {"own": (weights, mixing, cs, ds)}
+    for i, (turn, kinds_here) in enumerate(stops):
+        if i == FIRST_PAIR:
+            far = lax.ppermute(near, "sec", [(2 * t + k, 2 * t + 1 - k) for t in takers for k in range(2)])
+            mixing, cs, ds, weights = pl.pallas_call(
+                unpack_lent,
+                out_shape=tables,
+                in_specs=[VMEM] + [pl.BlockSpec(memory_space=pl.ANY)] * 2,
+                out_specs=(VMEM,) * 4,
+                scratch_shapes=[pltpu.SemaphoreType.DMA((2,))],
+                compiler_params=LIMIT,
+                name="unpack_lent",
+            )(lent_tables, near, far)
+            sets["lent"] = (weights, mixing, cs, ds)
         for c in range(CHUNKS):
-            chunks[c], kept = stage(turn, c, entries, coeffs, chunks[c], weights, mixing, cs, ds, kept)
-            if turn + 1 < chips:
-                chunks[c] = lax.ppermute(chunks[c], "sec", [(2 * turn + k, 2 * turn + 2 + k) for k in range(2)])
+            if len(kinds_here) > 1:
+                kept["own"], kept["lent"] = lax.optimization_barrier((kept["own"], kept["lent"]))
+            for kind in kinds_here:
+                last = i + 1 == len(stops) and kind == kinds_here[-1]
+                chunks[c], kept[kind] = stage(turn, c, entries, coeffs, last, chunks[c], *sets[kind], kept[kind])
+            if i + 1 < len(stops):
+                chunks[c] = lax.ppermute(chunks[c], "sec", [(2 * turn + k, 2 * stops[i + 1][0] + k) for k in range(2)])
+    kept["own"], kept["lent"] = lax.optimization_barrier((kept["own"], kept["lent"]))
+    back = lax.ppermute(kept["lent"], "sec", [(t, g) for g, t in to_taker])
+    kept = jnp.where(among(lax.axis_index("sec") // 2, givers), back, kept["own"])
 
     kept = kept.reshape(members, own_windows * ROWS, width)
     got = lax.all_to_all(kept, ("win", "sec"), 0, 0, axis_index_groups=groups, tiled=True)

time: 128 us -> 125 us (0.977)
  blocking collectives: 46.2 us -> 43.5 us
  waiting for transfers between devices: 51.1 us -> 53 us
  Pallas kernels: 7.41 us -> 6 us
    all_to_all x1, blocking collectives: 26.1 us -> 23.4 us  [local(): lax.all_to_all(kept, ('win', 'sec'), 0, 0, axis_index_groups=groups, tile...]
    ppermute x30 -> x28, waiting for transfers between devices: 51.1 us -> 53 us  [the longest x24 53 us: local(): lax.ppermute(chunks[c], 'sec', [(2 * turn + k, 2 * stops[i + 1][0] + k) f...]
    pallas_call x32 -> x33, Pallas kernels: 3.96 us -> 2.54 us  [the longest x32 2.5 us: stage(): pl.pallas_call(body, out_shape=(() if last else (sent,)) + (jax.ShapeDtyp...]
    ppermute x30 -> x28, starting transfers between devices: 21.2 us -> 20.3 us  [the longest x24 17.4 us: local(): lax.ppermute(chunks[c], 'sec', [(2 * turn + k, 2 * stops[i + 1][0] + k) f...]
  transfers between devices with their start and end apart: 31 -> 29, of which waited for: 2 -> 2; matrix products, arithmetic and copies ran while one was open for 0% -> 0% of each run, Pallas kernels for 3% -> 3%
where the time goes in v3:
time: 125 us; the launch traced here: 124 us
  waiting for transfers between devices  53 us (42%)
  blocking collectives  43.5 us (35%)
  starting transfers between devices  21 us (17%)
  Pallas kernels  6 us (5%)
    ppermute x24, waiting for transfers between devices, local(): lax.ppermute(chunks[c], 'sec', [(2 * turn + k, 2 * stops[i + 1][0] + k) f...  53 us
    all_to_all x1, blocking collectives, local(): lax.all_to_all(kept, ('win', 'sec'), 0, 0, axis_index_groups=groups, tile...  23.4 us
    all_to_all x1, blocking collectives, local(): lax.all_to_all(payload, ('win', 'sec'), 0, 0, axis_index_groups=groups, t...  20.1 us
    ppermute x24, starting transfers between devices, local(): lax.ppermute(chunks[c], 'sec', [(2 * turn + k, 2 * stops[i + 1][0] + k) f...  17.4 us
  transfers between devices with their start and end apart: 29, of which 2 were waited for; matrix products, arithmetic and copies ran while one was open for 0% of the time, Pallas kernels for 3%

profile of v3, /device:TPU:31, one launch (start us, length us, event | category | flops | bytes accessed | tf_op | source)
XLA Modules:
  0.0 124.3 jit_solution(4431306111840629217)
XLA Ops:
  0.0 0.7 collective-permute-start
  0.7 0.8 collective-permute-start.2
  1.5 1.8 %pack.1 = (bf16[16,16,512]{2,1,0:T(8,128)(2,1)S(1)}, bf16[2,4096,256]{2,1,0:T(8,128)(2,1)S(1)}) custom-call(bf16[5,2,24,512]{3,2,1,0:T(8,128)(2,1)} %initial_hbm.1, f32[1,2,256]{2,1,0:T(2,128)} %screen_hbm.1, s32[1,2,6]{2,1,0:T(2,128)} %links_hbm.1, s32[1,2,6]{2,1,0:T(2,128)} %kinds_hbm.1, s32[1,2]{1,0:T(1,128)} %counts_hbm.1, bf16[4096,256]{1,0:T(8,128)(2,1)} %bitcast.5), custom_call_target="tpu_custom_call" | custom-call | tf_op jit(solution)/shard_map/pack/pallas_call | solution.py:208
  3.3 20.1 %all_to_all.10.received_ref = bf16[16,16,512]{2,1,0:T(8,128)(2,1)S(1)} all-to-all(bf16[16,16,512]{2,1,0:T(8,128)(2,1)S(1)} %get-tuple-element.95), channel_id=1, replica_groups={{0,1,32,33,64,65,96,97,128,129,160,161,192,193,224,225},{2,3,34,35,66,6..., dimensions={0} | all-to-all | bytes 524288 | tf_op jit(solution)/shard_map/all_to_all | solution.py:227
  23.4 0.9 unpack.1
  24.3 0.7 collective-permute-start.1
  25.0 0.8 collective-permute-start.18
  25.8 0.7 collective-permute-start.4
  26.5 0.7 collective-permute-start.3
  27.3 0.7 collective-permute-start.6
  28.0 0.7 collective-permute-start.5
  28.7 0.7 collective-permute-start.8
  29.4 0.7 collective-permute-start.7
  30.1 0.7 collective-permute-start.10
  30.8 0.7 collective-permute-start.9
  31.5 0.7 collective-permute-start.12
  32.2 0.7 collective-permute-start.11
  33.0 0.7 collective-permute-start.14
  34.4 0.7 collective-permute-start.16
  35.1 0.7 collective-permute-start.15
  35.8 0.7 collective-permute-start.19
  38.1 0.8 collective-permute-start.20
  39.0 0.7 collective-permute-start.23
  41.9 1.3 %collective-permute-start.27 = (bf16[64,512]{1,0:T(8,128)(2,1)S(1)}, bf16[64,512]{1,0:T(8,128)(2,1)S(1)}, u32[]{:S(2)}, u32[]{:S(2)}) collective-permute-start(bf16[64,512]{1,0:T(8,128)(2,1)S(1)} %get-tuple-element.180), channel_id=1, source_target_pairs={{28,30},{29,31},{60,62},{61,63},{92,94},{93,95},{124,126},{125,127... | collective-permute-start | bytes 196616 | tf_op jit(solution)/shard_map/ppermute | solution.py:300
  43.3 1.3 %collective-permute-start.26 = (bf16[64,512]{1,0:T(8,128)(2,1)S(1)}, bf16[64,512]{1,0:T(8,128)(2,1)S(1)}, u32[]{:S(2)}, u32[]{:S(2)}) collective-permute-start(bf16[64,512]{1,0:T(8,128)(2,1)S(1)} %get-tuple-element.179), channel_id=1, source_target_pairs={{28,30},{29,31},{60,62},{61,63},{92,94},{93,95},{124,126},{125,127... | collective-permute-start | bytes 196616 | tf_op jit(solution)/shard_map/ppermute | solution.py:300
  44.6 49.8 %collective-permute-done.27.x_ref = bf16[64,512]{1,0:T(8,128)(2,1)S(1)} collective-permute-done((bf16[64,512]{1,0:T(8,128)(2,1)S(1)}, bf16[64,512]{1,0:T(8,128)(2,1)S(1)}, u32[]{:S(2)}, u32[]{:S(2)}) %collective-permute-start.27) | collective-permute-done | bytes 65568 | tf_op jit(solution)/shard_map/ppermute | solution.py:300
  94.4 0.9 stage.62.kept_ref
  95.3 3.2 %collective-permute-done.26.x_ref = bf16[64,512]{1,0:T(8,128)(2,1)S(1)} collective-permute-done((bf16[64,512]{1,0:T(8,128)(2,1)S(1)}, bf16[64,512]{1,0:T(8,128)(2,1)S(1)}, u32[]{:S(2)}, u32[]{:S(2)}) %collective-permute-start.26) | collective-permute-done | bytes 65568 | tf_op jit(solution)/shard_map/ppermute | solution.py:300
  98.5 0.9 stage.63
  99.4 0.7 collective-permute-start.28
  100.2 23.4 %all_to_all.11.got_ref = bf16[16,16,512]{2,1,0:T(8,128)(2,1)S(1)} all-to-all(bf16[16,16,512]{2,1,0:T(8,128)(2,1)S(1)} %bitcast.6), channel_id=1, replica_groups={{0,1,32,33,64,65,96,97,128,129,160,161,192,193,224,225},{2,3,34,35,66,6..., dimensions={0} | all-to-all | bytes 524288 | tf_op jit(solution)/shard_map/all_to_all | solution.py:306
  123.6 0.8 repack.1
  (67 shorter events, 4.8 us)
Async XLA Ops:
  0.0 23.4 %collective-permute-start = (bf16[4096,256]{1,0:T(8,128)(2,1)}, bf16[4096,256]{1,0:T(8,128)(2,1)S(1)}, u32[]{:S(2)}, u32[]{:S(2)}) collective-permute-start(bf16[4096,256]{1,0:T(8,128)(2,1)} %bitcast.3), channel_id=1, source_target_pairs={{0,1},{1,0},{2,3},{3,2},{4,5},{5,4},{6,7},{7,6},{8,9},{9,8},{10,11... | collective-permute-start | bytes 6291464 | tf_op jit(solution)/shard_map/ppermute | solution.py:202
  0.7 24.3 %collective-permute-start.2 = (bf16[4096,256]{1,0:T(8,128)(2,1)}, bf16[4096,256]{1,0:T(8,128)(2,1)S(1)}, u32[]{:S(2)}, u32[]{:S(2)}) collective-permute-start(bf16[4096,256]{1,0:T(8,128)(2,1)} %bitcast.4), channel_id=1, source_target_pairs={{16,18},{17,19},{22,20},{23,21},{24,26},{25,27},{48,50},{49,51},{5... | collective-permute-start | bytes 6291464 | tf_op jit(solution)/shard_map/ppermute | solution.py:206
  24.3 0.7 collective-permute-start.1
  25.0 12.2 %collective-permute-start.18 = (bf16[4096,256]{1,0:T(8,128)(2,1)S(1)}, bf16[4096,256]{1,0:T(8,128)(2,1)S(1)}, u32[]{:S(2)}, u32[]{:S(2)}) collective-permute-start(bf16[4096,256]{1,0:T(8,128)(2,1)S(1)} %collective-permute-done.2.near_ref), channel_id=1, source_target_pairs={{18,19},{19,18},{20,21},{21,20},{26,27},{27,26},{50,51},{51,50},{5... | collective-permute-start | bytes 6291464 | tf_op jit(solution)/shard_map/ppermute | solution.py:282
  25.8 1.4 %collective-permute-start.4 = (bf16[64,512]{1,0:T(8,128)(2,1)S(1)}, bf16[64,512]{1,0:T(8,128)(2,1)S(1)}, u32[]{:S(2)}, u32[]{:S(2)}) collective-permute-start(bf16[64,512]{1,0:T(8,128)(2,1)S(1)} %get-tuple-element.107), channel_id=1, source_target_pairs={{0,2},{1,3},{32,34},{33,35},{64,66},{65,67},{96,98},{97,99},{128,1... | collective-permute-start | bytes 196616 | tf_op jit(solution)/shard_map/ppermute | solution.py:300
  26.5 1.4 %collective-permute-start.3 = (bf16[64,512]{1,0:T(8,128)(2,1)S(1)}, bf16[64,512]{1,0:T(8,128)(2,1)S(1)}, u32[]{:S(2)}, u32[]{:S(2)}) collective-permute-start(bf16[64,512]{1,0:T(8,128)(2,1)S(1)} %get-tuple-element.106), channel_id=1, source_target_pairs={{0,2},{1,3},{32,34},{33,35},{64,66},{65,67},{96,98},{97,99},{128,1... | collective-permute-start | bytes 196616 | tf_op jit(solution)/shard_map/ppermute | solution.py:300
  27.3 1.4 %collective-permute-start.6 = (bf16[64,512]{1,0:T(8,128)(2,1)S(1)}, bf16[64,512]{1,0:T(8,128)(2,1)S(1)}, u32[]{:S(2)}, u32[]{:S(2)}) collective-permute-start(bf16[64,512]{1,0:T(8,128)(2,1)S(1)} %get-tuple-element.111), channel_id=1, source_target_pairs={{2,4},{3,5},{34,36},{35,37},{66,68},{67,69},{98,100},{99,101},{130... | collective-permute-start | bytes 196616 | tf_op jit(solution)/shard_map/ppermute | solution.py:300
  28.0 1.4 %collective-permute-start.5 = (bf16[64,512]{1,0:T(8,128)(2,1)S(1)}, bf16[64,512]{1,0:T(8,128)(2,1)S(1)}, u32[]{:S(2)}, u32[]{:S(2)}) collective-permute-start(bf16[64,512]{1,0:T(8,128)(2,1)S(1)} %get-tuple-element.110), channel_id=1, source_target_pairs={{2,4},{3,5},{34,36},{35,37},{66,68},{67,69},{98,100},{99,101},{130... | collective-permute-start | bytes 196616 | tf_op jit(solution)/shard_map/ppermute | solution.py:300
  28.7 1.4 %collective-permute-start.8 = (bf16[64,512]{1,0:T(8,128)(2,1)S(1)}, bf16[64,512]{1,0:T(8,128)(2,1)S(1)}, u32[]{:S(2)}, u32[]{:S(2)}) collective-permute-start(bf16[64,512]{1,0:T(8,128)(2,1)S(1)} %get-tuple-element.115), channel_id=1, source_target_pairs={{4,6},{5,7},{36,38},{37,39},{68,70},{69,71},{100,102},{101,103},{1... | collective-permute-start | bytes 196616 | tf_op jit(solution)/shard_map/ppermute | solution.py:300
  29.4 1.4 %collective-permute-start.7 = (bf16[64,512]{1,0:T(8,128)(2,1)S(1)}, bf16[64,512]{1,0:T(8,128)(2,1)S(1)}, u32[]{:S(2)}, u32[]{:S(2)}) collective-permute-start(bf16[64,512]{1,0:T(8,128)(2,1)S(1)} %get-tuple-element.114), channel_id=1, source_target_pairs={{4,6},{5,7},{36,38},{37,39},{68,70},{69,71},{100,102},{101,103},{1... | collective-permute-start | bytes 196616 | tf_op jit(solution)/shard_map/ppermute | solution.py:300
  30.1 1.4 %collective-permute-start.10 = (bf16[64,512]{1,0:T(8,128)(2,1)S(1)}, bf16[64,512]{1,0:T(8,128)(2,1)S(1)}, u32[]{:S(2)}, u32[]{:S(2)}) collective-permute-start(bf16[64,512]{1,0:T(8,128)(2,1)S(1)} %get-tuple-element.119), channel_id=1, source_target_pairs={{6,8},{7,9},{38,40},{39,41},{70,72},{71,73},{102,104},{103,105},{1... | collective-permute-start | bytes 196616 | tf_op jit(solution)/shard_map/ppermute | solution.py:300
  30.8 1.4 %collective-permute-start.9 = (bf16[64,512]{1,0:T(8,128)(2,1)S(1)}, bf16[64,512]{1,0:T(8,128)(2,1)S(1)}, u32[]{:S(2)}, u32[]{:S(2)}) collective-permute-start(bf16[64,512]{1,0:T(8,128)(2,1)S(1)} %get-tuple-element.118), channel_id=1, source_target_pairs={{6,8},{7,9},{38,40},{39,41},{70,72},{71,73},{102,104},{103,105},{1... | collective-permute-start | bytes 196616 | tf_op jit(solution)/shard_map/ppermute | solution.py:300
  31.5 1.4 %collective-permute-start.12 = (bf16[64,512]{1,0:T(8,128)(2,1)S(1)}, bf16[64,512]{1,0:T(8,128)(2,1)S(1)}, u32[]{:S(2)}, u32[]{:S(2)}) collective-permute-start(bf16[64,512]{1,0:T(8,128)(2,1)S(1)} %get-tuple-element.123), channel_id=1, source_target_pairs={{8,10},{9,11},{40,42},{41,43},{72,74},{73,75},{104,106},{105,107},... | collective-permute-start | bytes 196616 | tf_op jit(solution)/shard_map/ppermute | solution.py:300
  32.2 1.4 %collective-permute-start.11 = (bf16[64,512]{1,0:T(8,128)(2,1)S(1)}, bf16[64,512]{1,0:T(8,128)(2,1)S(1)}, u32[]{:S(2)}, u32[]{:S(2)}) collective-permute-start(bf16[64,512]{1,0:T(8,128)(2,1)S(1)} %get-tuple-element.122), channel_id=1, source_target_pairs={{8,10},{9,11},{40,42},{41,43},{72,74},{73,75},{104,106},{105,107},... | collective-permute-start | bytes 196616 | tf_op jit(solution)/shard_map/ppermute | solution.py:300
  33.0 1.4 %collective-permute-start.14 = (bf16[64,512]{1,0:T(8,128)(2,1)S(1)}, bf16[64,512]{1,0:T(8,128)(2,1)S(1)}, u32[]{:S(2)}, u32[]{:S(2)}) collective-permute-start(bf16[64,512]{1,0:T(8,128)(2,1)S(1)} %get-tuple-element.127), channel_id=1, source_target_pairs={{10,12},{11,13},{42,44},{43,45},{74,76},{75,77},{106,108},{107,109... | collective-permute-start | bytes 196616 | tf_op jit(solution)/shard_map/ppermute | solution.py:300
  33.7 1.4 %collective-permute-start.13 = (bf16[64,512]{1,0:T(8,128)(2,1)S(1)}, bf16[64,512]{1,0:T(8,128)(2,1)S(1)}, u32[]{:S(2)}, u32[]{:S(2)}) collective-permute-start(bf16[64,512]{1,0:T(8,128)(2,1)S(1)} %get-tuple-element.126), channel_id=1, source_target_pairs={{10,12},{11,13},{42,44},{43,45},{74,76},{75,77},{106,108},{107,109... | collective-permute-start | bytes 196616 | tf_op jit(solution)/shard_map/ppermute | solution.py:300
  34.4 1.4 %collective-permute-start.16 = (bf16[64,512]{1,0:T(8,128)(2,1)S(1)}, bf16[64,512]{1,0:T(8,128)(2,1)S(1)}, u32[]{:S(2)}, u32[]{:S(2)}) collective-permute-start(bf16[64,512]{1,0:T(8,128)(2,1)S(1)} %get-tuple-element.131), channel_id=1, source_target_pairs={{12,14},{13,15},{44,46},{45,47},{76,78},{77,79},{108,110},{109,111... | collective-permute-start | bytes 196616 | tf_op jit(solution)/shard_map/ppermute | solution.py:300
  35.1 1.4 %collective-permute-start.15 = (bf16[64,512]{1,0:T(8,128)(2,1)S(1)}, bf16[64,512]{1,0:T(8,128)(2,1)S(1)}, u32[]{:S(2)}, u32[]{:S(2)}) collective-permute-start(bf16[64,512]{1,0:T(8,128)(2,1)S(1)} %get-tuple-element.130), channel_id=1, source_target_pairs={{12,14},{13,15},{44,46},{45,47},{76,78},{77,79},{108,110},{109,111... | collective-permute-start | bytes 196616 | tf_op jit(solution)/shard_map/ppermute | solution.py:300
  35.8 1.4 %collective-permute-start.19 = (bf16[64,512]{1,0:T(8,128)(2,1)S(1)}, bf16[64,512]{1,0:T(8,128)(2,1)S(1)}, u32[]{:S(2)}, u32[]{:S(2)}) collective-permute-start(bf16[64,512]{1,0:T(8,128)(2,1)S(1)} %get-tuple-element.141), channel_id=1, source_target_pairs={{14,18},{15,19},{46,50},{47,51},{78,82},{79,83},{110,114},{111,115... | collective-permute-start | bytes 196616 | tf_op jit(solution)/shard_map/ppermute | solution.py:300
  36.5 1.5 %collective-permute-start.17 = (bf16[64,512]{1,0:T(8,128)(2,1)S(1)}, bf16[64,512]{1,0:T(8,128)(2,1)S(1)}, u32[]{:S(2)}, u32[]{:S(2)}) collective-permute-start(bf16[64,512]{1,0:T(8,128)(2,1)S(1)} %get-tuple-element.134), channel_id=1, source_target_pairs={{14,18},{15,19},{46,50},{47,51},{78,82},{79,83},{110,114},{111,115... | collective-permute-start | bytes 196616 | tf_op jit(solution)/shard_map/ppermute | solution.py:300
  37.3 1.6 %collective-permute-start.21 = (bf16[64,512]{1,0:T(8,128)(2,1)S(1)}, bf16[64,512]{1,0:T(8,128)(2,1)S(1)}, u32[]{:S(2)}, u32[]{:S(2)}) collective-permute-start(bf16[64,512]{1,0:T(8,128)(2,1)S(1)} %get-tuple-element.152), channel_id=1, source_target_pairs={{18,20},{19,21},{50,52},{51,53},{82,84},{83,85},{114,116},{115,117... | collective-permute-start | bytes 196616 | tf_op jit(solution)/shard_map/ppermute | solution.py:300
  38.1 1.6 %collective-permute-start.20 = (bf16[64,512]{1,0:T(8,128)(2,1)S(1)}, bf16[64,512]{1,0:T(8,128)(2,1)S(1)}, u32[]{:S(2)}, u32[]{:S(2)}) collective-permute-start(bf16[64,512]{1,0:T(8,128)(2,1)S(1)} %get-tuple-element.151), channel_id=1, source_target_pairs={{18,20},{19,21},{50,52},{51,53},{82,84},{83,85},{114,116},{115,117... | collective-permute-start | bytes 196616 | tf_op jit(solution)/shard_map/ppermute | solution.py:300
  39.0 1.4 %collective-permute-start.23 = (bf16[64,512]{1,0:T(8,128)(2,1)S(1)}, bf16[64,512]{1,0:T(8,128)(2,1)S(1)}, u32[]{:S(2)}, u32[]{:S(2)}) collective-permute-start(bf16[64,512]{1,0:T(8,128)(2,1)S(1)} %get-tuple-element.164), channel_id=1, source_target_pairs={{20,26},{21,27},{52,58},{53,59},{84,90},{85,91},{116,122},{117,123... | collective-permute-start | bytes 196616 | tf_op jit(solution)/shard_map/ppermute | solution.py:300
  39.8 1.4 %collective-permute-start.22 = (bf16[64,512]{1,0:T(8,128)(2,1)S(1)}, bf16[64,512]{1,0:T(8,128)(2,1)S(1)}, u32[]{:S(2)}, u32[]{:S(2)}) collective-permute-start(bf16[64,512]{1,0:T(8,128)(2,1)S(1)} %get-tuple-element.163), channel_id=1, source_target_pairs={{20,26},{21,27},{52,58},{53,59},{84,90},{85,91},{116,122},{117,123... | collective-permute-start | bytes 196616 | tf_op jit(solution)/shard_map/ppermute | solution.py:300
  40.5 1.4 %collective-permute-start.25 = (bf16[64,512]{1,0:T(8,128)(2,1)S(1)}, bf16[64,512]{1,0:T(8,128)(2,1)S(1)}, u32[]{:S(2)}, u32[]{:S(2)}) collective-permute-start(bf16[64,512]{1,0:T(8,128)(2,1)S(1)} %get-tuple-element.176), channel_id=1, source_target_pairs={{26,28},{27,29},{58,60},{59,61},{90,92},{91,93},{122,124},{123,125... | collective-permute-start | bytes 196616 | tf_op jit(solution)/shard_map/ppermute | solution.py:300
  41.2 2.0 %collective-permute-start.24 = (bf16[64,512]{1,0:T(8,128)(2,1)S(1)}, bf16[64,512]{1,0:T(8,128)(2,1)S(1)}, u32[]{:S(2)}, u32[]{:S(2)}) collective-permute-start(bf16[64,512]{1,0:T(8,128)(2,1)S(1)} %get-tuple-element.175), channel_id=1, source_target_pairs={{26,28},{27,29},{58,60},{59,61},{90,92},{91,93},{122,124},{123,125... | collective-permute-start | bytes 196616 | tf_op jit(solution)/shard_map/ppermute | solution.py:300
  41.9 52.4 %collective-permute-start.27 = (bf16[64,512]{1,0:T(8,128)(2,1)S(1)}, bf16[64,512]{1,0:T(8,128)(2,1)S(1)}, u32[]{:S(2)}, u32[]{:S(2)}) collective-permute-start(bf16[64,512]{1,0:T(8,128)(2,1)S(1)} %get-tuple-element.180), channel_id=1, source_target_pairs={{28,30},{29,31},{60,62},{61,63},{92,94},{93,95},{124,126},{125,127... | collective-permute-start | bytes 196616 | tf_op jit(solution)/shard_map/ppermute | solution.py:300
  43.3 55.2 %collective-permute-start.26 = (bf16[64,512]{1,0:T(8,128)(2,1)S(1)}, bf16[64,512]{1,0:T(8,128)(2,1)S(1)}, u32[]{:S(2)}, u32[]{:S(2)}) collective-permute-start(bf16[64,512]{1,0:T(8,128)(2,1)S(1)} %get-tuple-element.179), channel_id=1, source_target_pairs={{28,30},{29,31},{60,62},{61,63},{92,94},{93,95},{124,126},{125,127... | collective-permute-start | bytes 196616 | tf_op jit(solution)/shard_map/ppermute | solution.py:300
  99.4 0.7 collective-permute-start.28

commit v4 on v3

--- a/solution.py
+++ b/solution.py
@@ -275,7 +275,7 @@
         stops[-1][1].append(kind)
 
     kept = {kind: jnp.zeros((columns, 2, own_windows * ROWS, width), bf16) for kind in ("own", "lent")}
-    lent_tables, near, weights = lax.optimization_barrier((lent_tables, lent, weights))
+    near, weights = lax.optimization_barrier((lent, weights))
     sets = {"own": (weights, mixing, cs, ds)}
     for i, (turn, kinds_here) in enumerate(stops):
         if i == FIRST_PAIR:

time: 125 us -> 124 us (level)
  waiting for transfers between devices: 53 us -> 51.5 us
    ppermute x24, waiting for transfers between devices: 53 us -> 51.5 us  [local(): lax.ppermute(chunks[c], 'sec', [(2 * turn + k, 2 * stops[i + 1][0] + k) f...]
  transfers between devices with their start and end apart: 29 -> 29, of which waited for: 2 -> 2; matrix products, arithmetic and copies ran while one was open for 0% -> 0% of each run, Pallas kernels for 3% -> 4%
where the time goes in v4:
time: 124 us; the launch traced here: 123 us
  waiting for transfers between devices  51.5 us (42%)
  blocking collectives  43.5 us (35%)
  starting transfers between devices  21 us (17%)
  Pallas kernels  6 us (5%)
    ppermute x24, waiting for transfers between devices, local(): lax.ppermute(chunks[c], 'sec', [(2 * turn + k, 2 * stops[i + 1][0] + k) f...  51.5 us
    all_to_all x1, blocking collectives, local(): lax.all_to_all(kept, ('win', 'sec'), 0, 0, axis_index_groups=groups, tile...  23.4 us
    all_to_all x1, blocking collectives, local(): lax.all_to_all(payload, ('win', 'sec'), 0, 0, axis_index_groups=groups, t...  20.1 us
    ppermute x24, starting transfers between devices, local(): lax.ppermute(chunks[c], 'sec', [(2 * turn + k, 2 * stops[i + 1][0] + k) f...  17.4 us
    pallas_call x32, Pallas kernels, stage(): pl.pallas_call(body, out_shape=(() if last else (sent,)) + (jax.ShapeDtyp...  2.5 us
  transfers between devices with their start and end apart: 29, of which 2 were waited for; matrix products, arithmetic and copies ran while one was open for 0% of the time, Pallas kernels for 4%

profile of v4, /device:TPU:31, one launch (start us, length us, event | category | flops | bytes accessed | tf_op | source)
XLA Modules:
  0.0 122.8 jit_solution(1250642512156361416)
XLA Ops:
  0.0 0.7 collective-permute-start
  0.7 0.8 collective-permute-start.1
  1.5 1.8 %pack.1 = (bf16[16,16,512]{2,1,0:T(8,128)(2,1)S(1)}, bf16[2,4096,256]{2,1,0:T(8,128)(2,1)S(1)}) custom-call(bf16[5,2,24,512]{3,2,1,0:T(8,128)(2,1)} %initial_hbm.1, f32[1,2,256]{2,1,0:T(2,128)} %screen_hbm.1, s32[1,2,6]{2,1,0:T(2,128)} %links_hbm.1, s32[1,2,6]{2,1,0:T(2,128)} %kinds_hbm.1, s32[1,2]{1,0:T(1,128)} %counts_hbm.1, bf16[4096,256]{1,0:T(8,128)(2,1)} %bitcast.5), custom_call_target="tpu_custom_call" | custom-call | tf_op jit(solution)/shard_map/pack/pallas_call | solution.py:208
  3.3 20.1 %all_to_all.10.received_ref = bf16[16,16,512]{2,1,0:T(8,128)(2,1)S(1)} all-to-all(bf16[16,16,512]{2,1,0:T(8,128)(2,1)S(1)} %get-tuple-element.94), channel_id=1, replica_groups={{0,1,32,33,64,65,96,97,128,129,160,161,192,193,224,225},{2,3,34,35,66,6..., dimensions={0} | all-to-all | bytes 524288 | tf_op jit(solution)/shard_map/all_to_all | solution.py:227
  23.4 0.9 unpack.1
  24.3 0.8 collective-permute-start.18
  25.9 0.7 collective-permute-start.2
  26.6 0.7 collective-permute-start.5
  27.3 0.7 collective-permute-start.4
  28.0 0.7 collective-permute-start.7
  29.4 0.7 collective-permute-start.9
  30.1 0.7 collective-permute-start.8
  30.8 0.7 collective-permute-start.11
  32.3 0.7 collective-permute-start.13
  33.0 0.7 collective-permute-start.12
  33.7 0.7 collective-permute-start.15
  34.4 0.7 collective-permute-start.17
  35.1 0.7 collective-permute-start.14
  35.8 0.7 collective-permute-start.19
  36.5 0.7 collective-permute-start.16
  38.1 0.8 collective-permute-start.20
  39.0 0.7 collective-permute-start.23
  39.8 0.7 collective-permute-start.22
  41.9 1.3 %collective-permute-start.27 = (bf16[64,512]{1,0:T(8,128)(2,1)S(1)}, bf16[64,512]{1,0:T(8,128)(2,1)S(1)}, u32[]{:S(2)}, u32[]{:S(2)}) collective-permute-start(bf16[64,512]{1,0:T(8,128)(2,1)S(1)} %get-tuple-element.178), channel_id=1, source_target_pairs={{28,30},{29,31},{60,62},{61,63},{92,94},{93,95},{124,126},{125,127... | collective-permute-start | bytes 196616 | tf_op jit(solution)/shard_map/ppermute | solution.py:300
  43.3 1.3 %collective-permute-start.26 = (bf16[64,512]{1,0:T(8,128)(2,1)S(1)}, bf16[64,512]{1,0:T(8,128)(2,1)S(1)}, u32[]{:S(2)}, u32[]{:S(2)}) collective-permute-start(bf16[64,512]{1,0:T(8,128)(2,1)S(1)} %get-tuple-element.177), channel_id=1, source_target_pairs={{28,30},{29,31},{60,62},{61,63},{92,94},{93,95},{124,126},{125,127... | collective-permute-start | bytes 196616 | tf_op jit(solution)/shard_map/ppermute | solution.py:300
  44.6 48.3 %collective-permute-done.27.x_ref = bf16[64,512]{1,0:T(8,128)(2,1)S(1)} collective-permute-done((bf16[64,512]{1,0:T(8,128)(2,1)S(1)}, bf16[64,512]{1,0:T(8,128)(2,1)S(1)}, u32[]{:S(2)}, u32[]{:S(2)}) %collective-permute-start.27) | collective-permute-done | bytes 65568 | tf_op jit(solution)/shard_map/ppermute | solution.py:300
  92.9 0.9 stage.62.kept_ref
  93.8 3.2 %collective-permute-done.26.x_ref = bf16[64,512]{1,0:T(8,128)(2,1)S(1)} collective-permute-done((bf16[64,512]{1,0:T(8,128)(2,1)S(1)}, bf16[64,512]{1,0:T(8,128)(2,1)S(1)}, u32[]{:S(2)}, u32[]{:S(2)}) %collective-permute-start.26) | collective-permute-done | bytes 65568 | tf_op jit(solution)/shard_map/ppermute | solution.py:300
  97.0 0.9 stage.63
  97.9 0.7 collective-permute-start.28
  98.7 23.4 %all_to_all.11.got_ref = bf16[16,16,512]{2,1,0:T(8,128)(2,1)S(1)} all-to-all(bf16[16,16,512]{2,1,0:T(8,128)(2,1)S(1)} %bitcast.6), channel_id=1, replica_groups={{0,1,32,33,64,65,96,97,128,129,160,161,192,193,224,225},{2,3,34,35,66,6..., dimensions={0} | all-to-all | bytes 524288 | tf_op jit(solution)/shard_map/all_to_all | solution.py:306
  122.1 0.8 repack.1
  (67 shorter events, 4.8 us)
Async XLA Ops:
  0.0 23.4 %collective-permute-start = (bf16[4096,256]{1,0:T(8,128)(2,1)}, bf16[4096,256]{1,0:T(8,128)(2,1)S(1)}, u32[]{:S(2)}, u32[]{:S(2)}) collective-permute-start(bf16[4096,256]{1,0:T(8,128)(2,1)} %bitcast.3), channel_id=1, source_target_pairs={{0,1},{1,0},{2,3},{3,2},{4,5},{5,4},{6,7},{7,6},{8,9},{9,8},{10,11... | collective-permute-start | bytes 6291464 | tf_op jit(solution)/shard_map/ppermute | solution.py:202
  0.7 23.6 %collective-permute-start.1 = (bf16[4096,256]{1,0:T(8,128)(2,1)}, bf16[4096,256]{1,0:T(8,128)(2,1)S(1)}, u32[]{:S(2)}, u32[]{:S(2)}) collective-permute-start(bf16[4096,256]{1,0:T(8,128)(2,1)} %bitcast.4), channel_id=1, source_target_pairs={{16,18},{17,19},{22,20},{23,21},{24,26},{25,27},{48,50},{49,51},{5... | collective-permute-start | bytes 6291464 | tf_op jit(solution)/shard_map/ppermute | solution.py:206
  24.3 12.9 %collective-permute-start.18 = (bf16[4096,256]{1,0:T(8,128)(2,1)S(1)}, bf16[4096,256]{1,0:T(8,128)(2,1)S(1)}, u32[]{:S(2)}, u32[]{:S(2)}) collective-permute-start(bf16[4096,256]{1,0:T(8,128)(2,1)S(1)} %collective-permute-done.1.near_ref), channel_id=1, source_target_pairs={{18,19},{19,18},{20,21},{21,20},{26,27},{27,26},{50,51},{51,50},{5... | collective-permute-start | bytes 6291464 | tf_op jit(solution)/shard_map/ppermute | solution.py:282
  25.2 1.4 %collective-permute-start.3 = (bf16[64,512]{1,0:T(8,128)(2,1)S(1)}, bf16[64,512]{1,0:T(8,128)(2,1)S(1)}, u32[]{:S(2)}, u32[]{:S(2)}) collective-permute-start(bf16[64,512]{1,0:T(8,128)(2,1)S(1)} %get-tuple-element.105), channel_id=1, source_target_pairs={{0,2},{1,3},{32,34},{33,35},{64,66},{65,67},{96,98},{97,99},{128,1... | collective-permute-start | bytes 196616 | tf_op jit(solution)/shard_map/ppermute | solution.py:300
  25.9 1.4 %collective-permute-start.2 = (bf16[64,512]{1,0:T(8,128)(2,1)S(1)}, bf16[64,512]{1,0:T(8,128)(2,1)S(1)}, u32[]{:S(2)}, u32[]{:S(2)}) collective-permute-start(bf16[64,512]{1,0:T(8,128)(2,1)S(1)} %get-tuple-element.104), channel_id=1, source_target_pairs={{0,2},{1,3},{32,34},{33,35},{64,66},{65,67},{96,98},{97,99},{128,1... | collective-permute-start | bytes 196616 | tf_op jit(solution)/shard_map/ppermute | solution.py:300
  26.6 1.4 %collective-permute-start.5 = (bf16[64,512]{1,0:T(8,128)(2,1)S(1)}, bf16[64,512]{1,0:T(8,128)(2,1)S(1)}, u32[]{:S(2)}, u32[]{:S(2)}) collective-permute-start(bf16[64,512]{1,0:T(8,128)(2,1)S(1)} %get-tuple-element.109), channel_id=1, source_target_pairs={{2,4},{3,5},{34,36},{35,37},{66,68},{67,69},{98,100},{99,101},{130... | collective-permute-start | bytes 196616 | tf_op jit(solution)/shard_map/ppermute | solution.py:300
  27.3 1.4 %collective-permute-start.4 = (bf16[64,512]{1,0:T(8,128)(2,1)S(1)}, bf16[64,512]{1,0:T(8,128)(2,1)S(1)}, u32[]{:S(2)}, u32[]{:S(2)}) collective-permute-start(bf16[64,512]{1,0:T(8,128)(2,1)S(1)} %get-tuple-element.108), channel_id=1, source_target_pairs={{2,4},{3,5},{34,36},{35,37},{66,68},{67,69},{98,100},{99,101},{130... | collective-permute-start | bytes 196616 | tf_op jit(solution)/shard_map/ppermute | solution.py:300
  28.0 1.4 %collective-permute-start.7 = (bf16[64,512]{1,0:T(8,128)(2,1)S(1)}, bf16[64,512]{1,0:T(8,128)(2,1)S(1)}, u32[]{:S(2)}, u32[]{:S(2)}) collective-permute-start(bf16[64,512]{1,0:T(8,128)(2,1)S(1)} %get-tuple-element.113), channel_id=1, source_target_pairs={{4,6},{5,7},{36,38},{37,39},{68,70},{69,71},{100,102},{101,103},{1... | collective-permute-start | bytes 196616 | tf_op jit(solution)/shard_map/ppermute | solution.py:300
  28.7 1.4 %collective-permute-start.6 = (bf16[64,512]{1,0:T(8,128)(2,1)S(1)}, bf16[64,512]{1,0:T(8,128)(2,1)S(1)}, u32[]{:S(2)}, u32[]{:S(2)}) collective-permute-start(bf16[64,512]{1,0:T(8,128)(2,1)S(1)} %get-tuple-element.112), channel_id=1, source_target_pairs={{4,6},{5,7},{36,38},{37,39},{68,70},{69,71},{100,102},{101,103},{1... | collective-permute-start | bytes 196616 | tf_op jit(solution)/shard_map/ppermute | solution.py:300
  29.4 1.4 %collective-permute-start.9 = (bf16[64,512]{1,0:T(8,128)(2,1)S(1)}, bf16[64,512]{1,0:T(8,128)(2,1)S(1)}, u32[]{:S(2)}, u32[]{:S(2)}) collective-permute-start(bf16[64,512]{1,0:T(8,128)(2,1)S(1)} %get-tuple-element.117), channel_id=1, source_target_pairs={{6,8},{7,9},{38,40},{39,41},{70,72},{71,73},{102,104},{103,105},{1... | collective-permute-start | bytes 196616 | tf_op jit(solution)/shard_map/ppermute | solution.py:300
  30.1 1.4 %collective-permute-start.8 = (bf16[64,512]{1,0:T(8,128)(2,1)S(1)}, bf16[64,512]{1,0:T(8,128)(2,1)S(1)}, u32[]{:S(2)}, u32[]{:S(2)}) collective-permute-start(bf16[64,512]{1,0:T(8,128)(2,1)S(1)} %get-tuple-element.116), channel_id=1, source_target_pairs={{6,8},{7,9},{38,40},{39,41},{70,72},{71,73},{102,104},{103,105},{1... | collective-permute-start | bytes 196616 | tf_op jit(solution)/shard_map/ppermute | solution.py:300
  30.8 1.4 %collective-permute-start.11 = (bf16[64,512]{1,0:T(8,128)(2,1)S(1)}, bf16[64,512]{1,0:T(8,128)(2,1)S(1)}, u32[]{:S(2)}, u32[]{:S(2)}) collective-permute-start(bf16[64,512]{1,0:T(8,128)(2,1)S(1)} %get-tuple-element.121), channel_id=1, source_target_pairs={{8,10},{9,11},{40,42},{41,43},{72,74},{73,75},{104,106},{105,107},... | collective-permute-start | bytes 196616 | tf_op jit(solution)/shard_map/ppermute | solution.py:300
  31.6 1.4 %collective-permute-start.10 = (bf16[64,512]{1,0:T(8,128)(2,1)S(1)}, bf16[64,512]{1,0:T(8,128)(2,1)S(1)}, u32[]{:S(2)}, u32[]{:S(2)}) collective-permute-start(bf16[64,512]{1,0:T(8,128)(2,1)S(1)} %get-tuple-element.120), channel_id=1, source_target_pairs={{8,10},{9,11},{40,42},{41,43},{72,74},{73,75},{104,106},{105,107},... | collective-permute-start | bytes 196616 | tf_op jit(solution)/shard_map/ppermute | solution.py:300
  32.3 1.4 %collective-permute-start.13 = (bf16[64,512]{1,0:T(8,128)(2,1)S(1)}, bf16[64,512]{1,0:T(8,128)(2,1)S(1)}, u32[]{:S(2)}, u32[]{:S(2)}) collective-permute-start(bf16[64,512]{1,0:T(8,128)(2,1)S(1)} %get-tuple-element.125), channel_id=1, source_target_pairs={{10,12},{11,13},{42,44},{43,45},{74,76},{75,77},{106,108},{107,109... | collective-permute-start | bytes 196616 | tf_op jit(solution)/shard_map/ppermute | solution.py:300
  33.0 2.1 %collective-permute-start.12 = (bf16[64,512]{1,0:T(8,128)(2,1)S(1)}, bf16[64,512]{1,0:T(8,128)(2,1)S(1)}, u32[]{:S(2)}, u32[]{:S(2)}) collective-permute-start(bf16[64,512]{1,0:T(8,128)(2,1)S(1)} %get-tuple-element.124), channel_id=1, source_target_pairs={{10,12},{11,13},{42,44},{43,45},{74,76},{75,77},{106,108},{107,109... | collective-permute-start | bytes 196616 | tf_op jit(solution)/shard_map/ppermute | solution.py:300
  33.7 2.1 %collective-permute-start.15 = (bf16[64,512]{1,0:T(8,128)(2,1)S(1)}, bf16[64,512]{1,0:T(8,128)(2,1)S(1)}, u32[]{:S(2)}, u32[]{:S(2)}) collective-permute-start(bf16[64,512]{1,0:T(8,128)(2,1)S(1)} %get-tuple-element.129), channel_id=1, source_target_pairs={{12,14},{13,15},{44,46},{45,47},{76,78},{77,79},{108,110},{109,111... | collective-permute-start | bytes 196616 | tf_op jit(solution)/shard_map/ppermute | solution.py:300
  34.4 2.8 %collective-permute-start.17 = (bf16[16,8,512]{2,1,0:T(8,128)(2,1)S(1)}, bf16[16,8,512]{2,1,0:T(8,128)(2,1)S(1)}, u32[]{:S(2)}, u32[]{:S(2)}) collective-permute-start(bf16[16,8,512]{2,1,0:T(8,128)(2,1)S(1)} %get-tuple-element.133), channel_id=1, source_target_pairs={{16,18},{17,19},{22,20},{23,21},{24,26},{25,27},{48,50},{49,51},{5... | collective-permute-start | bytes 393224 | tf_op jit(solution)/shard_map/ppermute | solution.py:255
  35.1 1.4 %collective-permute-start.14 = (bf16[64,512]{1,0:T(8,128)(2,1)S(1)}, bf16[64,512]{1,0:T(8,128)(2,1)S(1)}, u32[]{:S(2)}, u32[]{:S(2)}) collective-permute-start(bf16[64,512]{1,0:T(8,128)(2,1)S(1)} %get-tuple-element.128), channel_id=1, source_target_pairs={{12,14},{13,15},{44,46},{45,47},{76,78},{77,79},{108,110},{109,111... | collective-permute-start | bytes 196616 | tf_op jit(solution)/shard_map/ppermute | solution.py:300
  35.8 1.5 %collective-permute-start.19 = (bf16[64,512]{1,0:T(8,128)(2,1)S(1)}, bf16[64,512]{1,0:T(8,128)(2,1)S(1)}, u32[]{:S(2)}, u32[]{:S(2)}) collective-permute-start(bf16[64,512]{1,0:T(8,128)(2,1)S(1)} %get-tuple-element.139), channel_id=1, source_target_pairs={{14,18},{15,19},{46,50},{47,51},{78,82},{79,83},{110,114},{111,115... | collective-permute-start | bytes 196616 | tf_op jit(solution)/shard_map/ppermute | solution.py:300
  36.5 1.5 %collective-permute-start.16 = (bf16[64,512]{1,0:T(8,128)(2,1)S(1)}, bf16[64,512]{1,0:T(8,128)(2,1)S(1)}, u32[]{:S(2)}, u32[]{:S(2)}) collective-permute-start(bf16[64,512]{1,0:T(8,128)(2,1)S(1)} %get-tuple-element.132), channel_id=1, source_target_pairs={{14,18},{15,19},{46,50},{47,51},{78,82},{79,83},{110,114},{111,115... | collective-permute-start | bytes 196616 | tf_op jit(solution)/shard_map/ppermute | solution.py:300
  37.3 1.6 %collective-permute-start.21 = (bf16[64,512]{1,0:T(8,128)(2,1)S(1)}, bf16[64,512]{1,0:T(8,128)(2,1)S(1)}, u32[]{:S(2)}, u32[]{:S(2)}) collective-permute-start(bf16[64,512]{1,0:T(8,128)(2,1)S(1)} %get-tuple-element.150), channel_id=1, source_target_pairs={{18,20},{19,21},{50,52},{51,53},{82,84},{83,85},{114,116},{115,117... | collective-permute-start | bytes 196616 | tf_op jit(solution)/shard_map/ppermute | solution.py:300
  38.1 1.6 %collective-permute-start.20 = (bf16[64,512]{1,0:T(8,128)(2,1)S(1)}, bf16[64,512]{1,0:T(8,128)(2,1)S(1)}, u32[]{:S(2)}, u32[]{:S(2)}) collective-permute-start(bf16[64,512]{1,0:T(8,128)(2,1)S(1)} %get-tuple-element.149), channel_id=1, source_target_pairs={{18,20},{19,21},{50,52},{51,53},{82,84},{83,85},{114,116},{115,117... | collective-permute-start | bytes 196616 | tf_op jit(solution)/shard_map/ppermute | solution.py:300
  39.0 1.4 %collective-permute-start.23 = (bf16[64,512]{1,0:T(8,128)(2,1)S(1)}, bf16[64,512]{1,0:T(8,128)(2,1)S(1)}, u32[]{:S(2)}, u32[]{:S(2)}) collective-permute-start(bf16[64,512]{1,0:T(8,128)(2,1)S(1)} %get-tuple-element.162), channel_id=1, source_target_pairs={{20,26},{21,27},{52,58},{53,59},{84,90},{85,91},{116,122},{117,123... | collective-permute-start | bytes 196616 | tf_op jit(solution)/shard_map/ppermute | solution.py:300
  39.8 1.4 %collective-permute-start.22 = (bf16[64,512]{1,0:T(8,128)(2,1)S(1)}, bf16[64,512]{1,0:T(8,128)(2,1)S(1)}, u32[]{:S(2)}, u32[]{:S(2)}) collective-permute-start(bf16[64,512]{1,0:T(8,128)(2,1)S(1)} %get-tuple-element.161), channel_id=1, source_target_pairs={{20,26},{21,27},{52,58},{53,59},{84,90},{85,91},{116,122},{117,123... | collective-permute-start | bytes 196616 | tf_op jit(solution)/shard_map/ppermute | solution.py:300
  40.5 1.4 %collective-permute-start.25 = (bf16[64,512]{1,0:T(8,128)(2,1)S(1)}, bf16[64,512]{1,0:T(8,128)(2,1)S(1)}, u32[]{:S(2)}, u32[]{:S(2)}) collective-permute-start(bf16[64,512]{1,0:T(8,128)(2,1)S(1)} %get-tuple-element.174), channel_id=1, source_target_pairs={{26,28},{27,29},{58,60},{59,61},{90,92},{91,93},{122,124},{123,125... | collective-permute-start | bytes 196616 | tf_op jit(solution)/shard_map/ppermute | solution.py:300
  41.2 2.0 %collective-permute-start.24 = (bf16[64,512]{1,0:T(8,128)(2,1)S(1)}, bf16[64,512]{1,0:T(8,128)(2,1)S(1)}, u32[]{:S(2)}, u32[]{:S(2)}) collective-permute-start(bf16[64,512]{1,0:T(8,128)(2,1)S(1)} %get-tuple-element.173), channel_id=1, source_target_pairs={{26,28},{27,29},{58,60},{59,61},{90,92},{91,93},{122,124},{123,125... | collective-permute-start | bytes 196616 | tf_op jit(solution)/shard_map/ppermute | solution.py:300
  41.9 50.9 %collective-permute-start.27 = (bf16[64,512]{1,0:T(8,128)(2,1)S(1)}, bf16[64,512]{1,0:T(8,128)(2,1)S(1)}, u32[]{:S(2)}, u32[]{:S(2)}) collective-permute-start(bf16[64,512]{1,0:T(8,128)(2,1)S(1)} %get-tuple-element.178), channel_id=1, source_target_pairs={{28,30},{29,31},{60,62},{61,63},{92,94},{93,95},{124,126},{125,127... | collective-permute-start | bytes 196616 | tf_op jit(solution)/shard_map/ppermute | solution.py:300
  43.3 53.7 %collective-permute-start.26 = (bf16[64,512]{1,0:T(8,128)(2,1)S(1)}, bf16[64,512]{1,0:T(8,128)(2,1)S(1)}, u32[]{:S(2)}, u32[]{:S(2)}) collective-permute-start(bf16[64,512]{1,0:T(8,128)(2,1)S(1)} %get-tuple-element.177), channel_id=1, source_target_pairs={{28,30},{29,31},{60,62},{61,63},{92,94},{93,95},{124,126},{125,127... | collective-permute-start | bytes 196616 | tf_op jit(solution)/shard_map/ppermute | solution.py:300
  97.9 0.7 collective-permute-start.28

commit v5 on v4

--- a/solution.py
+++ b/solution.py
@@ -19,7 +19,7 @@
 
 def pack_kernel(
     entries,
-    initial_hbm, screen_hbm, links_hbm, kinds_hbm, counts_hbm, own_hbm, out_ref, weights_ref,
+    initial_hbm, screen_hbm, links_hbm, kinds_hbm, counts_hbm, out_ref,
     initial_ref, screen_ref, links_ref, kinds_ref, counts_ref, sems,
 ):
     copies = [
@@ -31,13 +31,12 @@
                 (links_hbm, links_ref),
                 (screen_hbm, screen_ref),
                 (initial_hbm, initial_ref),
-                (own_hbm, weights_ref.at[lax.axis_index("sec") % 2]),
             )
         )
     ]
     for copy in copies:
         copy.start()
-    for copy in copies[:-1]:
+    for copy in copies:
         copy.wait()
     fronts, own_windows, sources, width = initial_ref.shape
     core = lax.axis_index("sec") % 2
@@ -68,7 +67,6 @@
         else:
             out_ref[member, :ROWS] = jnp.zeros((ROWS, width), jnp.bfloat16)
         out_ref[member, ROWS:] = tables
-    copies[-1].wait()
 
 
 def unpack_kernel(entries, coeffs, received_ref, tables_at, placed, field_refs, mix_ref, cs_ref, ds_ref, weights_ref, sems):
@@ -205,36 +203,34 @@
     to_taker = [(2 * g + k, 2 * t + k) for t, g in lend for k in range(2)]
     lent = lax.ppermute(own, "sec", to_taker)
 
-    payload, weights = pl.pallas_call(
+    payload = pl.pallas_call(
         functools.partial(pack_kernel, entries),
-        out_shape=(
-            jax.ShapeDtypeStruct((members, 2 * ROWS, width), bf16),
-            jax.ShapeDtypeStruct((2,) + own.shape, bf16),
-        ),
-        in_specs=[HBM] * 6,
-        out_specs=(VMEM, VMEM),
+        out_shape=jax.ShapeDtypeStruct((members, 2 * ROWS, width), bf16),
+        in_specs=[HBM] * 5,
+        out_specs=VMEM,
         scratch_shapes=[
             pltpu.VMEM(initial.shape, initial.dtype),
             pltpu.VMEM(screen.shape, screen.dtype),
             pltpu.SMEM(links.shape, links.dtype),
             pltpu.SMEM(kinds.shape, kinds.dtype),
             pltpu.SMEM(counts.shape, counts.dtype),
-            pltpu.SemaphoreType.DMA((6,)),
+            pltpu.SemaphoreType.DMA((5,)),
         ],
         compiler_params=LIMIT,
         name="pack",
-    )(*[pltpu.with_memory_space_constraint(a, pltpu.HBM) for a in (initial, screen, links, kinds, counts, own)])
+    )(*[pltpu.with_memory_space_constraint(a, pltpu.HBM) for a in (initial, screen, links, kinds, counts)])
     received = lax.all_to_all(payload, ("win", "sec"), 0, 0, axis_index_groups=groups, tiled=True)
     part = points // CHUNKS
     tables = (
         jax.ShapeDtypeStruct((2, 3 * entries, part, LANES), f32),
         jax.ShapeDtypeStruct((2, part, coeffs), f32),
         jax.ShapeDtypeStruct((2, part, coeffs), f32),
-        jax.ShapeDtypeStruct(weights.shape, bf16),
+        jax.ShapeDtypeStruct((2,) + own.shape, bf16),
     )
 
-    def unpack(received_ref, other_ref, weights_in_ref, *refs):
-        placed = [(other_ref, 1 - lax.axis_index("sec") % 2)]
+    def unpack(received_ref, other_ref, own_ref, *refs):
+        core = lax.axis_index("sec") % 2
+        placed = [(own_ref, core), (other_ref, 1 - core)]
         for member in range(members):
             refs[-2][member] = received_ref[member, ROWS:]
         unpack_kernel(entries, coeffs, received_ref, ROWS, placed, refs[:CHUNKS], *refs[CHUNKS:-2], refs[-1])
@@ -244,13 +240,12 @@
         out_shape=(jax.ShapeDtypeStruct((part, width), bf16),) * CHUNKS
         + tables
         + (jax.ShapeDtypeStruct((members, ROWS, width), bf16),),
-        in_specs=[VMEM] * 3,
+        in_specs=[VMEM, VMEM, HBM],
         out_specs=(VMEM,) * (5 + CHUNKS),
-        scratch_shapes=[pltpu.SemaphoreType.DMA((1,))],
-        input_output_aliases={2: 3 + CHUNKS},
+        scratch_shapes=[pltpu.SemaphoreType.DMA((2,))],
         compiler_params=LIMIT,
         name="unpack",
-    )(received, other, weights)
+    )(received, other, pltpu.with_memory_space_constraint(own, pltpu.HBM))
 
     lent_tables = lax.ppermute(lent_tables, "sec", to_taker)
 

time: 124 us -> 124 us (level)
  no operation moved by 1% of the time
where the time goes in v5:
time: 124 us; the launch traced here: 123 us
  waiting for transfers between devices  51.5 us (42%)
  blocking collectives  43.5 us (35%)
  starting transfers between devices  21 us (17%)
  Pallas kernels  6 us (5%)
    ppermute x24, waiting for transfers between devices, local(): lax.ppermute(chunks[c], 'sec', [(2 * turn + k, 2 * stops[i + 1][0] + k) f...  51.5 us
    all_to_all x1, blocking collectives, local(): lax.all_to_all(kept, ('win', 'sec'), 0, 0, axis_index_groups=groups, tile...  23.4 us
    all_to_all x1, blocking collectives, local(): lax.all_to_all(payload, ('win', 'sec'), 0, 0, axis_index_groups=groups, t...  20.1 us
    ppermute x24, starting transfers between devices, local(): lax.ppermute(chunks[c], 'sec', [(2 * turn + k, 2 * stops[i + 1][0] + k) f...  17.4 us
    pallas_call x32, Pallas kernels, stage(): pl.pallas_call(body, out_shape=(() if last else (sent,)) + (jax.ShapeDtyp...  2.49 us
  transfers between devices with their start and end apart: 29, of which 2 were waited for; matrix products, arithmetic and copies ran while one was open for 0% of the time, Pallas kernels for 4%

profile of v5, /device:TPU:31, one launch (start us, length us, event | category | flops | bytes accessed | tf_op | source)
XLA Modules:
  0.0 122.8 jit_solution(10822835551428364943)
XLA Ops:
  0.0 0.7 collective-permute-start
  0.7 0.8 collective-permute-start.1
  1.5 1.1 pack.1
  2.6 20.1 %all_to_all.10.received_ref = bf16[16,16,512]{2,1,0:T(8,128)(2,1)S(1)} all-to-all(bf16[16,16,512]{2,1,0:T(8,128)(2,1)S(1)} %pack.1), channel_id=1, replica_groups={{0,1,32,33,64,65,96,97,128,129,160,161,192,193,224,225},{2,3,34,35,66,6..., dimensions={0} | all-to-all | bytes 524288 | tf_op jit(solution)/shard_map/all_to_all | solution.py:222
  22.7 1.6 %unpack.1 = (bf16[64,512]{1,0:T(8,128)(2,1)S(1)}, bf16[64,512]{1,0:T(8,128)(2,1)S(1)}, f32[2,24,64,128]{3,2,1,0:T(8,128)S(1)}, f32[2,64,256]{2,1,0:T(8,128)S(1)}...) custom-call(bf16[16,16,512]{2,1,0:T(8,128)(2,1)S(1)} %all_to_all.10.received_ref, ...), custom_call_target="tpu_custom_call" | custom-call | tf_op jit(solution)/shard_map/unpack/pallas_call | solution.py:238
  24.3 0.8 collective-permute-start.18
  25.2 0.7 collective-permute-start.3
  26.6 0.7 collective-permute-start.5
  27.3 0.7 collective-permute-start.4
  28.0 0.7 collective-permute-start.7
  28.7 0.7 collective-permute-start.6
  29.4 0.7 collective-permute-start.9
  30.1 0.7 collective-permute-start.8
  30.9 0.7 collective-permute-start.11
  31.6 0.7 collective-permute-start.10
  32.3 0.7 collective-permute-start.13
  33.0 0.7 collective-permute-start.12
  34.4 0.7 collective-permute-start.17
  35.1 0.7 collective-permute-start.14
  35.8 0.7 collective-permute-start.19
  36.5 0.7 collective-permute-start.16
  37.4 0.7 collective-permute-start.21
  38.1 0.8 collective-permute-start.20
  42.0 1.3 %collective-permute-start.27 = (bf16[64,512]{1,0:T(8,128)(2,1)S(1)}, bf16[64,512]{1,0:T(8,128)(2,1)S(1)}, u32[]{:S(2)}, u32[]{:S(2)}) collective-permute-start(bf16[64,512]{1,0:T(8,128)(2,1)S(1)} %get-tuple-element.174), channel_id=1, source_target_pairs={{28,30},{29,31},{60,62},{61,63},{92,94},{93,95},{124,126},{125,127... | collective-permute-start | bytes 196616 | tf_op jit(solution)/shard_map/ppermute | solution.py:295
  43.3 1.3 %collective-permute-start.26 = (bf16[64,512]{1,0:T(8,128)(2,1)S(1)}, bf16[64,512]{1,0:T(8,128)(2,1)S(1)}, u32[]{:S(2)}, u32[]{:S(2)}) collective-permute-start(bf16[64,512]{1,0:T(8,128)(2,1)S(1)} %get-tuple-element.173), channel_id=1, source_target_pairs={{28,30},{29,31},{60,62},{61,63},{92,94},{93,95},{124,126},{125,127... | collective-permute-start | bytes 196616 | tf_op jit(solution)/shard_map/ppermute | solution.py:295
  44.6 48.3 %collective-permute-done.27.x_ref = bf16[64,512]{1,0:T(8,128)(2,1)S(1)} collective-permute-done((bf16[64,512]{1,0:T(8,128)(2,1)S(1)}, bf16[64,512]{1,0:T(8,128)(2,1)S(1)}, u32[]{:S(2)}, u32[]{:S(2)}) %collective-permute-start.27) | collective-permute-done | bytes 65568 | tf_op jit(solution)/shard_map/ppermute | solution.py:295
  92.9 0.9 stage.62.kept_ref
  93.8 3.1 %collective-permute-done.26.x_ref = bf16[64,512]{1,0:T(8,128)(2,1)S(1)} collective-permute-done((bf16[64,512]{1,0:T(8,128)(2,1)S(1)}, bf16[64,512]{1,0:T(8,128)(2,1)S(1)}, u32[]{:S(2)}, u32[]{:S(2)}) %collective-permute-start.26) | collective-permute-done | bytes 65568 | tf_op jit(solution)/shard_map/ppermute | solution.py:295
  96.9 0.9 stage.63
  97.9 0.7 collective-permute-start.28
  98.6 23.4 %all_to_all.11.got_ref = bf16[16,16,512]{2,1,0:T(8,128)(2,1)S(1)} all-to-all(bf16[16,16,512]{2,1,0:T(8,128)(2,1)S(1)} %bitcast.6), channel_id=1, replica_groups={{0,1,32,33,64,65,96,97,128,129,160,161,192,193,224,225},{2,3,34,35,66,6..., dimensions={0} | all-to-all | bytes 524288 | tf_op jit(solution)/shard_map/all_to_all | solution.py:301
  122.1 0.8 repack.1
  (67 shorter events, 4.8 us)
Async XLA Ops:
  0.0 22.7 %collective-permute-start = (bf16[4096,256]{1,0:T(8,128)(2,1)}, bf16[4096,256]{1,0:T(8,128)(2,1)S(1)}, u32[]{:S(2)}, u32[]{:S(2)}) collective-permute-start(bf16[4096,256]{1,0:T(8,128)(2,1)} %bitcast.3), channel_id=1, source_target_pairs={{0,1},{1,0},{2,3},{3,2},{4,5},{5,4},{6,7},{7,6},{8,9},{9,8},{10,11... | collective-permute-start | bytes 6291464 | tf_op jit(solution)/shard_map/ppermute | solution.py:200
  0.7 23.6 %collective-permute-start.1 = (bf16[4096,256]{1,0:T(8,128)(2,1)}, bf16[4096,256]{1,0:T(8,128)(2,1)S(1)}, u32[]{:S(2)}, u32[]{:S(2)}) collective-permute-start(bf16[4096,256]{1,0:T(8,128)(2,1)} %bitcast.4), channel_id=1, source_target_pairs={{16,18},{17,19},{22,20},{23,21},{24,26},{25,27},{48,50},{49,51},{5... | collective-permute-start | bytes 6291464 | tf_op jit(solution)/shard_map/ppermute | solution.py:204
  24.3 12.9 %collective-permute-start.18 = (bf16[4096,256]{1,0:T(8,128)(2,1)S(1)}, bf16[4096,256]{1,0:T(8,128)(2,1)S(1)}, u32[]{:S(2)}, u32[]{:S(2)}) collective-permute-start(bf16[4096,256]{1,0:T(8,128)(2,1)S(1)} %collective-permute-done.1.near_ref), channel_id=1, source_target_pairs={{18,19},{19,18},{20,21},{21,20},{26,27},{27,26},{50,51},{51,50},{5... | collective-permute-start | bytes 6291464 | tf_op jit(solution)/shard_map/ppermute | solution.py:277
  25.2 1.4 %collective-permute-start.3 = (bf16[64,512]{1,0:T(8,128)(2,1)S(1)}, bf16[64,512]{1,0:T(8,128)(2,1)S(1)}, u32[]{:S(2)}, u32[]{:S(2)}) collective-permute-start(bf16[64,512]{1,0:T(8,128)(2,1)S(1)} %get-tuple-element.101), channel_id=1, source_target_pairs={{0,2},{1,3},{32,34},{33,35},{64,66},{65,67},{96,98},{97,99},{128,1... | collective-permute-start | bytes 196616 | tf_op jit(solution)/shard_map/ppermute | solution.py:295
  25.9 1.4 %collective-permute-start.2 = (bf16[64,512]{1,0:T(8,128)(2,1)S(1)}, bf16[64,512]{1,0:T(8,128)(2,1)S(1)}, u32[]{:S(2)}, u32[]{:S(2)}) collective-permute-start(bf16[64,512]{1,0:T(8,128)(2,1)S(1)} %get-tuple-element.100), channel_id=1, source_target_pairs={{0,2},{1,3},{32,34},{33,35},{64,66},{65,67},{96,98},{97,99},{128,1... | collective-permute-start | bytes 196616 | tf_op jit(solution)/shard_map/ppermute | solution.py:295
  26.6 1.4 %collective-permute-start.5 = (bf16[64,512]{1,0:T(8,128)(2,1)S(1)}, bf16[64,512]{1,0:T(8,128)(2,1)S(1)}, u32[]{:S(2)}, u32[]{:S(2)}) collective-permute-start(bf16[64,512]{1,0:T(8,128)(2,1)S(1)} %get-tuple-element.105), channel_id=1, source_target_pairs={{2,4},{3,5},{34,36},{35,37},{66,68},{67,69},{98,100},{99,101},{130... | collective-permute-start | bytes 196616 | tf_op jit(solution)/shard_map/ppermute | solution.py:295
  27.3 1.4 %collective-permute-start.4 = (bf16[64,512]{1,0:T(8,128)(2,1)S(1)}, bf16[64,512]{1,0:T(8,128)(2,1)S(1)}, u32[]{:S(2)}, u32[]{:S(2)}) collective-permute-start(bf16[64,512]{1,0:T(8,128)(2,1)S(1)} %get-tuple-element.104), channel_id=1, source_target_pairs={{2,4},{3,5},{34,36},{35,37},{66,68},{67,69},{98,100},{99,101},{130... | collective-permute-start | bytes 196616 | tf_op jit(solution)/shard_map/ppermute | solution.py:295
  28.0 1.4 %collective-permute-start.7 = (bf16[64,512]{1,0:T(8,128)(2,1)S(1)}, bf16[64,512]{1,0:T(8,128)(2,1)S(1)}, u32[]{:S(2)}, u32[]{:S(2)}) collective-permute-start(bf16[64,512]{1,0:T(8,128)(2,1)S(1)} %get-tuple-element.109), channel_id=1, source_target_pairs={{4,6},{5,7},{36,38},{37,39},{68,70},{69,71},{100,102},{101,103},{1... | collective-permute-start | bytes 196616 | tf_op jit(solution)/shard_map/ppermute | solution.py:295
  28.7 1.4 %collective-permute-start.6 = (bf16[64,512]{1,0:T(8,128)(2,1)S(1)}, bf16[64,512]{1,0:T(8,128)(2,1)S(1)}, u32[]{:S(2)}, u32[]{:S(2)}) collective-permute-start(bf16[64,512]{1,0:T(8,128)(2,1)S(1)} %get-tuple-element.108), channel_id=1, source_target_pairs={{4,6},{5,7},{36,38},{37,39},{68,70},{69,71},{100,102},{101,103},{1... | collective-permute-start | bytes 196616 | tf_op jit(solution)/shard_map/ppermute | solution.py:295
  29.4 1.4 %collective-permute-start.9 = (bf16[64,512]{1,0:T(8,128)(2,1)S(1)}, bf16[64,512]{1,0:T(8,128)(2,1)S(1)}, u32[]{:S(2)}, u32[]{:S(2)}) collective-permute-start(bf16[64,512]{1,0:T(8,128)(2,1)S(1)} %get-tuple-element.113), channel_id=1, source_target_pairs={{6,8},{7,9},{38,40},{39,41},{70,72},{71,73},{102,104},{103,105},{1... | collective-permute-start | bytes 196616 | tf_op jit(solution)/shard_map/ppermute | solution.py:295
  30.1 1.4 %collective-permute-start.8 = (bf16[64,512]{1,0:T(8,128)(2,1)S(1)}, bf16[64,512]{1,0:T(8,128)(2,1)S(1)}, u32[]{:S(2)}, u32[]{:S(2)}) collective-permute-start(bf16[64,512]{1,0:T(8,128)(2,1)S(1)} %get-tuple-element.112), channel_id=1, source_target_pairs={{6,8},{7,9},{38,40},{39,41},{70,72},{71,73},{102,104},{103,105},{1... | collective-permute-start | bytes 196616 | tf_op jit(solution)/shard_map/ppermute | solution.py:295
  30.9 1.4 %collective-permute-start.11 = (bf16[64,512]{1,0:T(8,128)(2,1)S(1)}, bf16[64,512]{1,0:T(8,128)(2,1)S(1)}, u32[]{:S(2)}, u32[]{:S(2)}) collective-permute-start(bf16[64,512]{1,0:T(8,128)(2,1)S(1)} %get-tuple-element.117), channel_id=1, source_target_pairs={{8,10},{9,11},{40,42},{41,43},{72,74},{73,75},{104,106},{105,107},... | collective-permute-start | bytes 196616 | tf_op jit(solution)/shard_map/ppermute | solution.py:295
  31.6 1.4 %collective-permute-start.10 = (bf16[64,512]{1,0:T(8,128)(2,1)S(1)}, bf16[64,512]{1,0:T(8,128)(2,1)S(1)}, u32[]{:S(2)}, u32[]{:S(2)}) collective-permute-start(bf16[64,512]{1,0:T(8,128)(2,1)S(1)} %get-tuple-element.116), channel_id=1, source_target_pairs={{8,10},{9,11},{40,42},{41,43},{72,74},{73,75},{104,106},{105,107},... | collective-permute-start | bytes 196616 | tf_op jit(solution)/shard_map/ppermute | solution.py:295
  32.3 1.4 %collective-permute-start.13 = (bf16[64,512]{1,0:T(8,128)(2,1)S(1)}, bf16[64,512]{1,0:T(8,128)(2,1)S(1)}, u32[]{:S(2)}, u32[]{:S(2)}) collective-permute-start(bf16[64,512]{1,0:T(8,128)(2,1)S(1)} %get-tuple-element.121), channel_id=1, source_target_pairs={{10,12},{11,13},{42,44},{43,45},{74,76},{75,77},{106,108},{107,109... | collective-permute-start | bytes 196616 | tf_op jit(solution)/shard_map/ppermute | solution.py:295
  33.0 2.1 %collective-permute-start.12 = (bf16[64,512]{1,0:T(8,128)(2,1)S(1)}, bf16[64,512]{1,0:T(8,128)(2,1)S(1)}, u32[]{:S(2)}, u32[]{:S(2)}) collective-permute-start(bf16[64,512]{1,0:T(8,128)(2,1)S(1)} %get-tuple-element.120), channel_id=1, source_target_pairs={{10,12},{11,13},{42,44},{43,45},{74,76},{75,77},{106,108},{107,109... | collective-permute-start | bytes 196616 | tf_op jit(solution)/shard_map/ppermute | solution.py:295
  33.7 2.1 %collective-permute-start.15 = (bf16[64,512]{1,0:T(8,128)(2,1)S(1)}, bf16[64,512]{1,0:T(8,128)(2,1)S(1)}, u32[]{:S(2)}, u32[]{:S(2)}) collective-permute-start(bf16[64,512]{1,0:T(8,128)(2,1)S(1)} %get-tuple-element.125), channel_id=1, source_target_pairs={{12,14},{13,15},{44,46},{45,47},{76,78},{77,79},{108,110},{109,111... | collective-permute-start | bytes 196616 | tf_op jit(solution)/shard_map/ppermute | solution.py:295
  34.4 2.8 %collective-permute-start.17 = (bf16[16,8,512]{2,1,0:T(8,128)(2,1)S(1)}, bf16[16,8,512]{2,1,0:T(8,128)(2,1)S(1)}, u32[]{:S(2)}, u32[]{:S(2)}) collective-permute-start(bf16[16,8,512]{2,1,0:T(8,128)(2,1)S(1)} %get-tuple-element.129), channel_id=1, source_target_pairs={{16,18},{17,19},{22,20},{23,21},{24,26},{25,27},{48,50},{49,51},{5... | collective-permute-start | bytes 393224 | tf_op jit(solution)/shard_map/ppermute | solution.py:250
  35.1 1.4 %collective-permute-start.14 = (bf16[64,512]{1,0:T(8,128)(2,1)S(1)}, bf16[64,512]{1,0:T(8,128)(2,1)S(1)}, u32[]{:S(2)}, u32[]{:S(2)}) collective-permute-start(bf16[64,512]{1,0:T(8,128)(2,1)S(1)} %get-tuple-element.124), channel_id=1, source_target_pairs={{12,14},{13,15},{44,46},{45,47},{76,78},{77,79},{108,110},{109,111... | collective-permute-start | bytes 196616 | tf_op jit(solution)/shard_map/ppermute | solution.py:295
  35.8 1.5 %collective-permute-start.19 = (bf16[64,512]{1,0:T(8,128)(2,1)S(1)}, bf16[64,512]{1,0:T(8,128)(2,1)S(1)}, u32[]{:S(2)}, u32[]{:S(2)}) collective-permute-start(bf16[64,512]{1,0:T(8,128)(2,1)S(1)} %get-tuple-element.135), channel_id=1, source_target_pairs={{14,18},{15,19},{46,50},{47,51},{78,82},{79,83},{110,114},{111,115... | collective-permute-start | bytes 196616 | tf_op jit(solution)/shard_map/ppermute | solution.py:295
  36.5 1.5 %collective-permute-start.16 = (bf16[64,512]{1,0:T(8,128)(2,1)S(1)}, bf16[64,512]{1,0:T(8,128)(2,1)S(1)}, u32[]{:S(2)}, u32[]{:S(2)}) collective-permute-start(bf16[64,512]{1,0:T(8,128)(2,1)S(1)} %get-tuple-element.128), channel_id=1, source_target_pairs={{14,18},{15,19},{46,50},{47,51},{78,82},{79,83},{110,114},{111,115... | collective-permute-start | bytes 196616 | tf_op jit(solution)/shard_map/ppermute | solution.py:295
  37.4 1.6 %collective-permute-start.21 = (bf16[64,512]{1,0:T(8,128)(2,1)S(1)}, bf16[64,512]{1,0:T(8,128)(2,1)S(1)}, u32[]{:S(2)}, u32[]{:S(2)}) collective-permute-start(bf16[64,512]{1,0:T(8,128)(2,1)S(1)} %get-tuple-element.146), channel_id=1, source_target_pairs={{18,20},{19,21},{50,52},{51,53},{82,84},{83,85},{114,116},{115,117... | collective-permute-start | bytes 196616 | tf_op jit(solution)/shard_map/ppermute | solution.py:295
  38.1 1.6 %collective-permute-start.20 = (bf16[64,512]{1,0:T(8,128)(2,1)S(1)}, bf16[64,512]{1,0:T(8,128)(2,1)S(1)}, u32[]{:S(2)}, u32[]{:S(2)}) collective-permute-start(bf16[64,512]{1,0:T(8,128)(2,1)S(1)} %get-tuple-element.145), channel_id=1, source_target_pairs={{18,20},{19,21},{50,52},{51,53},{82,84},{83,85},{114,116},{115,117... | collective-permute-start | bytes 196616 | tf_op jit(solution)/shard_map/ppermute | solution.py:295
  39.0 1.4 %collective-permute-start.23 = (bf16[64,512]{1,0:T(8,128)(2,1)S(1)}, bf16[64,512]{1,0:T(8,128)(2,1)S(1)}, u32[]{:S(2)}, u32[]{:S(2)}) collective-permute-start(bf16[64,512]{1,0:T(8,128)(2,1)S(1)} %get-tuple-element.158), channel_id=1, source_target_pairs={{20,26},{21,27},{52,58},{53,59},{84,90},{85,91},{116,122},{117,123... | collective-permute-start | bytes 196616 | tf_op jit(solution)/shard_map/ppermute | solution.py:295
  39.8 1.4 %collective-permute-start.22 = (bf16[64,512]{1,0:T(8,128)(2,1)S(1)}, bf16[64,512]{1,0:T(8,128)(2,1)S(1)}, u32[]{:S(2)}, u32[]{:S(2)}) collective-permute-start(bf16[64,512]{1,0:T(8,128)(2,1)S(1)} %get-tuple-element.157), channel_id=1, source_target_pairs={{20,26},{21,27},{52,58},{53,59},{84,90},{85,91},{116,122},{117,123... | collective-permute-start | bytes 196616 | tf_op jit(solution)/shard_map/ppermute | solution.py:295
  40.5 1.4 %collective-permute-start.25 = (bf16[64,512]{1,0:T(8,128)(2,1)S(1)}, bf16[64,512]{1,0:T(8,128)(2,1)S(1)}, u32[]{:S(2)}, u32[]{:S(2)}) collective-permute-start(bf16[64,512]{1,0:T(8,128)(2,1)S(1)} %get-tuple-element.170), channel_id=1, source_target_pairs={{26,28},{27,29},{58,60},{59,61},{90,92},{91,93},{122,124},{123,125... | collective-permute-start | bytes 196616 | tf_op jit(solution)/shard_map/ppermute | solution.py:295
  41.2 2.0 %collective-permute-start.24 = (bf16[64,512]{1,0:T(8,128)(2,1)S(1)}, bf16[64,512]{1,0:T(8,128)(2,1)S(1)}, u32[]{:S(2)}, u32[]{:S(2)}) collective-permute-start(bf16[64,512]{1,0:T(8,128)(2,1)S(1)} %get-tuple-element.169), channel_id=1, source_target_pairs={{26,28},{27,29},{58,60},{59,61},{90,92},{91,93},{122,124},{123,125... | collective-permute-start | bytes 196616 | tf_op jit(solution)/shard_map/ppermute | solution.py:295
  42.0 50.9 %collective-permute-start.27 = (bf16[64,512]{1,0:T(8,128)(2,1)S(1)}, bf16[64,512]{1,0:T(8,128)(2,1)S(1)}, u32[]{:S(2)}, u32[]{:S(2)}) collective-permute-start(bf16[64,512]{1,0:T(8,128)(2,1)S(1)} %get-tuple-element.174), channel_id=1, source_target_pairs={{28,30},{29,31},{60,62},{61,63},{92,94},{93,95},{124,126},{125,127... | collective-permute-start | bytes 196616 | tf_op jit(solution)/shard_map/ppermute | solution.py:295
  43.3 53.7 %collective-permute-start.26 = (bf16[64,512]{1,0:T(8,128)(2,1)S(1)}, bf16[64,512]{1,0:T(8,128)(2,1)S(1)}, u32[]{:S(2)}, u32[]{:S(2)}) collective-permute-start(bf16[64,512]{1,0:T(8,128)(2,1)S(1)} %get-tuple-element.173), channel_id=1, source_target_pairs={{28,30},{29,31},{60,62},{61,63},{92,94},{93,95},{124,126},{125,127... | collective-permute-start | bytes 196616 | tf_op jit(solution)/shard_map/ppermute | solution.py:295
  97.9 0.7 collective-permute-start.28
